TPU v7x, 512 devices: a whole 4x8x8 slice. The times are simulated.
512 devices in a mesh: lon: 64 (over y_hi, z, core), lat: 8 (over y_lo, x).
Axes of the slice: x: 4, y: 8 (y_hi: 4, y_lo: 2; y = y_hi * 2 + y_lo), z: 8, core: 2. Of those that a mesh axis runs over, the one named last changes fastest.
Arguments:
- field_in: bfloat16 [4, 96, 147456], P(None, 'lat', 'lon'), may hold values from -6 to 6
- norm1_gain: float32 [192], replicated, may hold values from 0.25 to 1.75
- qkv_weight: bfloat16 [192, 576], replicated, may hold values from -0.4375 to 0.4375
- proj_weight: bfloat16 [192, 192], replicated, may hold values from -0.4375 to 0.4375
- earth_bias: float32 [16, 2, 6, 20736], P('lat'), may hold values from -4 to 320, as said below
- norm2_gain: float32 [192], replicated, may hold values from 0.25 to 1.75
- fc1_weight: bfloat16 [192, 768], replicated, may hold values from -0.4375 to 0.4375
- fc2_weight: bfloat16 [768, 192], replicated, may hold values from -0.21875 to 0.21875
Outputs:
- block_out: bfloat16 [4, 96, 147456], P(None, 'lat', 'lon')
Inputs may be any that keep to these rules, and one draw needn't show every extreme that they name: `earth_bias`: bias table entries.
All inputs are finite; a program needn't handle non-finite values.
Results may differ from a plain program's by a relative error of at most 0.014.
Values may be sent and summed in bfloat16 or wider, within the bound.
A program may use at most 128 MiB of HBM per device.

v0:
```python
import jax
import jax.numpy as jnp
from jax import lax
from jax.sharding import PartitionSpec as P

WIN_LEV = 2
WIN_LAT = 6
WIN_LON = 12


def shifted(x, axis, by):
    devices = lax.axis_size(axis)
    return lax.ppermute(x, axis, [(i, (i + by) % devices) for i in range(devices)])


def row_regions(orig, total):
    tail = 2
    edge = WIN_LAT // 2
    return jnp.where(
        orig < 0,
        3,
        jnp.where(
            orig < edge, 2, jnp.where(orig < total - edge, 0, jnp.where(orig < total, 1, tail))
        ),
    )


def level_regions(levels):
    place = jnp.arange(levels)
    return jnp.where(place < levels - 2, 0, jnp.where(place == levels - 2, 1, 2))


def layer_norm(values, gain):
    center = values - jnp.mean(values, axis=-1, keepdims=True)
    spread = jnp.mean(center * center, axis=-1, keepdims=True)
    return center * lax.rsqrt(spread + 1e-05) * gain


def attend(tile, gain, qkv_weight, proj_weight, bias_types, level_lab, row_lab):
    levels, rows, flat = tile.shape
    chans = qkv_weight.shape[0]
    cols = flat // chans
    heads = bias_types.shape[2]
    head_dim = chans // heads
    zwin = levels // WIN_LEV
    rwin = rows // WIN_LAT
    cwin = cols // WIN_LON
    tokens = WIN_LEV * WIN_LAT * WIN_LON
    grid = tile.reshape(zwin, WIN_LEV, rwin, WIN_LAT, cwin, WIN_LON, chans)
    windows = grid.transpose(0, 2, 4, 1, 3, 5, 6).reshape(-1, chans)
    normed = layer_norm(windows.astype(jnp.float32), gain).astype(jnp.bfloat16)
    qkv = jnp.dot(normed, qkv_weight, preferred_element_type=jnp.float32).astype(jnp.bfloat16)
    qkv = qkv.reshape(zwin, rwin, cwin, tokens, 3, heads, head_dim)
    query = qkv[:, :, :, :, 0]
    keys = qkv[:, :, :, :, 1]
    values = qkv[:, :, :, :, 2]
    scores = jnp.einsum(
        "abcqhd,abckhd->bachqk", query, keys, preferred_element_type=jnp.float32
    ) * head_dim ** (-0.5)
    table = bias_types.reshape(rwin, zwin, heads, tokens, tokens)
    scores = scores + table[:, :, None]
    zlab = level_lab.reshape(zwin, WIN_LEV)
    rlab = row_lab.reshape(rwin, WIN_LAT)
    label = (
        zlab[None, :, :, None, None] * 8
        + rlab[:, None, None, :, None]
        + jnp.zeros((1, 1, 1, 1, WIN_LON), jnp.int32)
    )
    label = label.reshape(rwin, zwin, tokens)
    allowed = label[:, :, :, None] == label[:, :, None, :]
    scores = jnp.where(allowed[:, :, None, None], scores, -1000000000.0)
    probs = jax.nn.softmax(scores, axis=-1).astype(jnp.bfloat16)
    mixed = jnp.einsum("bachqk,abckhd->abcqhd", probs, values, preferred_element_type=jnp.float32)
    mixed = mixed.astype(jnp.bfloat16).reshape(-1, chans)
    proj = jnp.dot(mixed, proj_weight, preferred_element_type=jnp.float32).astype(jnp.bfloat16)
    back = proj.reshape(zwin, rwin, cwin, WIN_LEV, WIN_LAT, WIN_LON, chans).transpose(
        0, 3, 1, 4, 2, 5, 6
    )
    return back.reshape(levels, rows, flat)


def finish(tile, attn, gain, fc1_weight, fc2_weight):
    chans = fc1_weight.shape[0]
    resid = (tile.astype(jnp.float32) + attn.astype(jnp.float32)).astype(jnp.bfloat16)
    resid = lax.optimization_barrier(resid).reshape(-1, chans)
    normed = layer_norm(resid.astype(jnp.float32), gain).astype(jnp.bfloat16)
    hidden = jax.nn.gelu(jnp.dot(normed, fc1_weight, preferred_element_type=jnp.float32)).astype(
        jnp.bfloat16
    )
    result = resid.astype(jnp.float32) + jnp.dot(
        hidden, fc2_weight, preferred_element_type=jnp.float32
    )
    return result.astype(jnp.bfloat16).reshape(tile.shape)


def shards(
    field_in, norm1_gain, qkv_weight, proj_weight, earth_bias, norm2_gain, fc1_weight, fc2_weight
):
    levels, rows, flat = field_in.shape
    chans = qkv_weight.shape[0]
    half_lanes = WIN_LON // 2 * chans
    edge = WIN_LAT // 2
    total_rows = rows * lax.axis_size("lat")
    lat_place = lax.axis_index("lat")
    level_lab = level_regions(levels)
    incoming = shifted(field_in[:, :, :half_lanes], "lon", -1)
    tile = jnp.concatenate([field_in[:, :, half_lanes:], incoming], axis=2)
    above = shifted(tile[:, :edge], "lat", -1)
    tile = jnp.concatenate([tile[:, edge:], above], axis=1)
    tile = jnp.roll(tile, -1, axis=0)
    orig = lat_place * rows + edge + jnp.arange(rows)
    row_lab = row_regions(orig, total_rows)
    attn = attend(tile, norm1_gain, qkv_weight, proj_weight, earth_bias, level_lab, row_lab)
    done = jnp.roll(finish(tile, attn, norm2_gain, fc1_weight, fc2_weight), 1, axis=0)
    below = shifted(done[:, rows - edge :], "lat", 1)
    done = jnp.concatenate([below, done[:, : rows - edge]], axis=1)
    western = shifted(done[:, :, flat - half_lanes :], "lon", 1)
    return jnp.concatenate([western, done[:, :, : flat - half_lanes]], axis=2)


def solution(mesh):
    in_specs = (P(None, "lat", "lon"), P(), P(), P(), P("lat", None, None, None), P(), P(), P())
    out_specs = P(None, "lat", "lon")
    return jax.shard_map(shards, mesh=mesh, in_specs=in_specs, out_specs=out_specs, check_vma=False)
```

profile of v0, /device:TPU:8, one launch (start us, length us, event | category | flops | bytes accessed | tf_op | source)
XLA Modules:
  0.0 72.8 jit_solution(3434560118164878618)
XLA Ops:
  0.0 1.1 %fusion.45 = (bf16[4,12,1152]{2,0,1:T(4,128)(2,1)S(1)}, bf16[4,12,1152]{2,0,1:T(4,128)(2,1)S(1)}) fusion(bf16[4,12,2304]{2,0,1:T(4,128)(2,1)} %param.8), kind=kLoop, calls=%fused_computation.75 | loop fusion | bytes 442368 | tf_op jit(solution)/shard_map/slice | solution.py:107
  1.1 13.2 %collective-permute-start = (bf16[4,12,1152]{2,0,1:T(4,128)(2,1)S(1)}, bf16[4,12,1152]{2,0,1:T(4,128)(2,1)S(1)}, u32[]{:S(2)}, u32[]{:S(2)}) collective-permute-start(bf16[4,12,1152]{2,0,1:T(4,128)(2,1)S(1)} %get-tuple-element.9), channel_id=1, source_target_pairs={{0,504},{8,0},{16,8},{24,16},{32,24},{40,32},{48,40},{56,48},{64,5... | collective-permute-start | bytes 331784 | tf_op jit(solution)/shard_map/ppermute | solution.py:13
  14.5 0.8 %broadcast_compare_fusion = pred[2,2,144,144]{2,3,1,0:T(8,128)(4,1)} fusion(s32[2,2,144]{2,1,0:T(2,128)S(1)} %eq.28), kind=kLoop, calls=%fused_computation.42 | loop fusion | flops 82944 | bytes 85248 | tf_op jit(solution)/shard_map/eq | solution.py:70
  15.4 5.2 %broadcast_in_dim_reshape.2 = f32[2,2,6,144,144]{4,3,1,2,0:T(8,128)} reshape(f32[2,2,6,20736]{3,1,2,0:T(2,128)} %param.12) | data formatting | bytes 3981312 | tf_op jit(solution)/shard_map/broadcast_in_dim;reshape | solution.py:61
  20.5 5.6 %copy.37 = f32[2,2,6,144,144]{3,4,2,1,0:T(8,128)} copy(f32[2,2,6,144,144]{4,3,1,2,0:T(8,128)} %broadcast_in_dim_reshape.2) | data formatting | bytes 3981312 | tf_op jit(solution)/shard_map/broadcast_in_dim;reshape | solution.py:61
  26.2 5.6 %collective-permute-start.1 = (bf16[4,3,2304]{2,0,1:T(4,128)(2,1)S(1)}, bf16[4,3,2304]{2,0,1:T(4,128)(2,1)S(1)}, u32[]{:S(2)}, u32[]{:S(2)}) collective-permute-start(bf16[4,3,2304]{2,0,1:T(4,128)(2,1)S(1)} %pad_maximum_fusion.2), channel_id=1, source_target_pairs={{0,7},{1,0},{2,1},{3,2},{4,3},{5,4},{6,5},{7,6},{8,15},{9,8},{10,9... | collective-permute-start | bytes 165896 | tf_op jit(solution)/shard_map/ppermute | solution.py:13
  31.9 1.5 %collective-permute-done.1 = bf16[4,3,2304]{2,0,1:T(4,128)(2,1)S(1)} collective-permute-done((bf16[4,3,2304]{2,0,1:T(4,128)(2,1)S(1)}, bf16[4,3,2304]{2,0,1:T(4,128)(2,1)S(1)}, u32[]{:S(2)}, u32[]{:S(2)}) %collective-permute-start.1) | collective-permute-done | bytes 55328 | tf_op jit(solution)/shard_map/ppermute | solution.py:13
  33.8 0.4 reshape.166
  34.2 0.2 bitcast_reduce_fusion
  34.5 0.4 multiply_reduce_fusion
  35.4 0.5 convolution_convert_fusion
  35.9 0.4 copy.33
  36.3 0.8 %reshape.157 = bf16[2,2,1,144,3,6,32]{3,1,0,6,5,4,2:T(2,128)(2,1)S(1)} reshape(bf16[576,576]{0,1:T(8,128)(2,1)S(1)} %copy.33) | data formatting | bytes 1327104 | tf_op jit(solution)/shard_map/reshape | solution.py:53
  37.1 1.0 %fusion.44 = (bf16[2,2,1,144,1,6,32]{3,1,0,6,5,4,2:T(2,128)(2,1)S(1)}, bf16[2,2,1,144,1,6,32]{3,1,0,6,5,4,2:T(2,128)(2,1)S(1)}, bf16[2,2,1,144,1,6,32]{3,1,0,6,5,4,2:T(2,128)(2,1)S(1)}) fusion(bf16[2,2,1,144,3,6,32]{3,1,0,6,5,4,2:T(2,128)(2,1)S(1)} %reshape.157), kind=kLoop, calls=%fused_computation.74 | loop fusion | bytes 1327104 | tf_op jit(solution)/shard_map/slice | solution.py:56
  38.1 5.4 %fusion.46 = (f32[2,2,6,144]{3,2,1,0:T(8,128)S(1)}, f32[2,2,6,144,144]{3,4,2,1,0:T(8,128)}) fusion(f32[2,2,6,144,144]{3,4,2,1,0:T(8,128)} %copy.37, pred[2,2,144,144]{2,3,1,0:T(8,128)(4,1)S(1)} %copy-done.2, bf16[2,2,1,144,1,6,32]{3,1,0,6,5,4,2:T(2,128)(2,1)S(1)} %get-tuple-element.6, bf16[2,2,1,144,1,6,32]{3,1,0,6,5,4,2:T(2,128)(2,1)S(1)} %get-tuple-element.7), kind=kOutput, calls=%fused_computation.76 | convolution fusion | flops 34338960 | bytes 4520448 | tf_op jit(solution)/shard_map/sub | solution.py:72
  43.5 2.4 %fusion.16 = bf16[2,2,1,144,6,32]{3,5,4,1,0,2:T(8,128)(2,1)S(1)} fusion(bf16[2,2,1,144,1,6,32]{3,1,0,6,5,4,2:T(2,128)(2,1)S(1)} %get-tuple-element.5, f32[2,2,6,144,144]{3,4,2,1,0:T(8,128)} %get-tuple-element.11, f32[2,2,6,144]{3,2,1,0:T(8,128)S(1)} %get-tuple-element.10), kind=kOutput, calls=%fused_computation.19 | convolution fusion | flops 32956416 | bytes 2446848 | tf_op jit(solution)/shard_map/bachqk,abckhd->abcqhd/dot_general | solution.py:73
  45.9 0.4 copy.39
  46.3 0.2 reshape.161
  46.6 0.3 fusion.20
  46.9 0.2 copy.40
  47.2 0.4 reshape.163
  47.6 0.3 add_convert_fusion
  48.0 0.3 reshape.164
  48.3 0.2 copy.43
  48.7 0.3 multiply_reduce_fusion.1
  49.0 1.0 %fusion.19 = bf16[576,192]{0,1:T(8,128)(2,1)S(1)} fusion(f32[576,192]{0,1:T(8,128)S(1)} %copy.43, bf16[768,192]{0,1:T(8,128)(2,1)S(1)} %copy-done, bf16[192,768]{1,0:T(8,128)(2,1)S(1)} %copy-done.5, f32[576,192]{1,0:T(8,128)S(1)} %reshape.164, f32[192]{0:T(256)S(1)} %copy-done.6, f32[576]{0:T(1024)S(1)} %add_rsqrt_fusion.1, ...), kind=kOutput, calls=%fused_computation.20 | convolution fusion | flops 344383488 | bytes 1701120 | tf_op jit(solution)/shard_map/dot_general | solution.py:90
  50.6 0.3 slice.67
  50.9 2.2 %collective-permute-start.2 = (bf16[4,3,2304]{2,1,0:T(4,128)(2,1)S(1)}, bf16[4,3,2304]{2,1,0:T(4,128)(2,1)S(1)}, u32[]{:S(2)}, u32[]{:S(2)}) collective-permute-start(bf16[4,3,2304]{2,1,0:T(4,128)(2,1)S(1)} %slice.81), channel_id=1, source_target_pairs={{0,1},{1,2},{2,3},{3,4},{4,5},{5,6},{6,7},{7,0},{8,9},{9,10},{10,1... | collective-permute-start | bytes 165896 | tf_op jit(solution)/shard_map/ppermute | solution.py:13
  53.1 6.5 %collective-permute-done.2 = bf16[4,3,2304]{2,1,0:T(4,128)(2,1)S(1)} collective-permute-done((bf16[4,3,2304]{2,1,0:T(4,128)(2,1)S(1)}, bf16[4,3,2304]{2,1,0:T(4,128)(2,1)S(1)}, u32[]{:S(2)}, u32[]{:S(2)}) %collective-permute-start.2) | collective-permute-done | bytes 55328 | tf_op jit(solution)/shard_map/ppermute | solution.py:13
  59.7 1.9 %collective-permute-start.3 = (bf16[4,12,1152]{2,1,0:T(8,128)(2,1)S(1)}, bf16[4,12,1152]{2,1,0:T(8,128)(2,1)S(1)}, u32[]{:S(2)}, u32[]{:S(2)}) collective-permute-start(bf16[4,12,1152]{2,1,0:T(8,128)(2,1)S(1)} %fusion.38), channel_id=1, source_target_pairs={{0,8},{8,16},{16,24},{24,32},{32,40},{40,48},{48,56},{56,64},{64,7... | collective-permute-start | bytes 331784 | tf_op jit(solution)/shard_map/ppermute | solution.py:13
  61.6 10.3 %collective-permute-done.3 = bf16[4,12,1152]{2,1,0:T(8,128)(2,1)S(1)} collective-permute-done((bf16[4,12,1152]{2,1,0:T(8,128)(2,1)S(1)}, bf16[4,12,1152]{2,1,0:T(8,128)(2,1)S(1)}, u32[]{:S(2)}, u32[]{:S(2)}) %collective-permute-start.3) | collective-permute-done | bytes 110624 | tf_op jit(solution)/shard_map/ppermute | solution.py:13
  72.0 0.8 %copy.46 = bf16[4,12,2304]{2,0,1:T(4,128)(2,1)} copy(bf16[4,12,2304]{2,1,0:T(8,128)(2,1)S(1)} %fusion.25) | data formatting | bytes 442368 | tf_op jit(solution)/shard_map/concatenate | solution.py:118
  (48 shorter events, 2.3 us)
Async XLA Ops:
  0.0 49.0 %copy-start = (bf16[768,192]{0,1:T(8,128)(2,1)S(1)}, bf16[768,192]{0,1:T(8,128)(2,1)}, u32[]{:S(2)}) copy-start(bf16[768,192]{0,1:T(8,128)(2,1)} %param.15) | copy-start | bytes 884740
  1.1 25.0 %collective-permute-start = (bf16[4,12,1152]{2,0,1:T(4,128)(2,1)S(1)}, bf16[4,12,1152]{2,0,1:T(4,128)(2,1)S(1)}, u32[]{:S(2)}, u32[]{:S(2)}) collective-permute-start(bf16[4,12,1152]{2,0,1:T(4,128)(2,1)S(1)} %get-tuple-element.9), channel_id=1, source_target_pairs={{0,504},{8,0},{16,8},{24,16},{32,24},{40,32},{48,40},{56,48},{64,5... | collective-permute-start | bytes 331784 | tf_op jit(solution)/shard_map/ppermute | solution.py:13
  26.2 7.2 %collective-permute-start.1 = (bf16[4,3,2304]{2,0,1:T(4,128)(2,1)S(1)}, bf16[4,3,2304]{2,0,1:T(4,128)(2,1)S(1)}, u32[]{:S(2)}, u32[]{:S(2)}) collective-permute-start(bf16[4,3,2304]{2,0,1:T(4,128)(2,1)S(1)} %pad_maximum_fusion.2), channel_id=1, source_target_pairs={{0,7},{1,0},{2,1},{3,2},{4,3},{5,4},{6,5},{7,6},{8,15},{9,8},{10,9... | collective-permute-start | bytes 165896 | tf_op jit(solution)/shard_map/ppermute | solution.py:13
  34.5 0.9 %copy-start.1 = (bf16[192,576]{1,0:T(8,128)(2,1)S(1)}, bf16[192,576]{1,0:T(8,128)(2,1)}, u32[]{:S(2)}) copy-start(bf16[192,576]{1,0:T(8,128)(2,1)} %param.10) | copy-start | bytes 663556
  34.5 0.9 %copy-start.4 = (f32[192]{0:T(256)S(1)}, f32[192]{0:T(256)}, u32[]{:S(2)}) copy-start(f32[192]{0:T(256)} %param.9) | copy-start | bytes 2308
  37.1 1.0 %copy-start.2 = (pred[2,2,144,144]{2,3,1,0:T(8,128)(4,1)S(1)}, pred[2,2,144,144]{2,3,1,0:T(8,128)(4,1)}, u32[]{:S(2)}) copy-start(pred[2,2,144,144]{2,3,1,0:T(8,128)(4,1)} %broadcast_compare_fusion) | copy-start | bytes 248836
  43.5 3.1 %copy-start.3 = (bf16[192,192]{1,0:T(8,128)(2,1)S(1)}, bf16[192,192]{1,0:T(8,128)(2,1)}, u32[]{:S(2)}) copy-start(bf16[192,192]{1,0:T(8,128)(2,1)} %param.11) | copy-start | bytes 221188
  47.9 1.1 %copy-start.5 = (bf16[192,768]{1,0:T(8,128)(2,1)S(1)}, bf16[192,768]{1,0:T(8,128)(2,1)}, u32[]{:S(2)}) copy-start(bf16[192,768]{1,0:T(8,128)(2,1)} %param.14) | copy-start | bytes 884740
  47.9 1.1 %copy-start.6 = (f32[192]{0:T(256)S(1)}, f32[192]{0:T(256)}, u32[]{:S(2)}) copy-start(f32[192]{0:T(256)} %param.13) | copy-start | bytes 2308
  50.9 8.7 %collective-permute-start.2 = (bf16[4,3,2304]{2,1,0:T(4,128)(2,1)S(1)}, bf16[4,3,2304]{2,1,0:T(4,128)(2,1)S(1)}, u32[]{:S(2)}, u32[]{:S(2)}) collective-permute-start(bf16[4,3,2304]{2,1,0:T(4,128)(2,1)S(1)} %slice.81), channel_id=1, source_target_pairs={{0,1},{1,2},{2,3},{3,4},{4,5},{5,6},{6,7},{7,0},{8,9},{9,10},{10,1... | collective-permute-start | bytes 165896 | tf_op jit(solution)/shard_map/ppermute | solution.py:13
  59.7 12.2 %collective-permute-start.3 = (bf16[4,12,1152]{2,1,0:T(8,128)(2,1)S(1)}, bf16[4,12,1152]{2,1,0:T(8,128)(2,1)S(1)}, u32[]{:S(2)}, u32[]{:S(2)}) collective-permute-start(bf16[4,12,1152]{2,1,0:T(8,128)(2,1)S(1)} %fusion.38), channel_id=1, source_target_pairs={{0,8},{8,16},{16,24},{24,32},{32,40},{40,48},{48,56},{56,64},{64,7... | collective-permute-start | bytes 331784 | tf_op jit(solution)/shard_map/ppermute | solution.py:13
where the time goes:
time: 73.1 us; the launch traced here: 72.8 us
  starting transfers between devices  22.9 us (31%)
  local copies, waits for them, and re-layouts  18.6 us (25%)
  waiting for transfers between devices  18.3 us (25%)
  matrix products  9.59 us (13%)
  other arithmetic  2.9 us (4%)
    ppermute x4, starting transfers between devices, shifted(): lax.ppermute(x, axis, [(i, (i + by) % devices) for i in range(devices)])  22.9 us
    ppermute x4, waiting for transfers between devices, shifted(): lax.ppermute(x, axis, [(i, (i + by) % devices) for i in range(devices)])  18.3 us
    another operation x2, local copies, waits for them, and re-layouts, attend(): scores = scores + table[:, :, None]  10.8 us
    sub x1, matrix products, attend(): probs = jax.nn.softmax(scores, axis=-1).astype(jnp.bfloat16)  5.37 us
    dot_general x1, matrix products, attend(): jnp.einsum('bachqk,abckhd->abcqhd', probs, values, preferred_element_type...  2.39 us
  transfers between devices with their start and end apart: 4, of which 3 were waited for; matrix products, arithmetic and copies ran while one was open for 16% of the time, Pallas kernels for 0%

commit v1 on v0

v1 whole, which is shorter than its diff:
```python
import functools

import jax
import jax.numpy as jnp
from jax import lax
from jax.experimental import pallas as pl
from jax.experimental.pallas import tpu as pltpu
from jax.sharding import PartitionSpec as P

MESH = pl.DeviceIdType.MESH
BF16 = jnp.bfloat16
F32 = jnp.float32
CH = 192
HEADS = 6
HD = CH // HEADS
TOK = 144
HALF = TOK // 2
LEVEL = ((1, 2), (3, 0))
NEG = -1000000000.0


def dot_nt(a, b):
    return lax.dot_general(a, b, (((1,), (1,)), ((), ())), preferred_element_type=F32)


def dot(a, b):
    return jnp.dot(a, b, preferred_element_type=F32)


def layer_norm(values, gain):
    center = values - jnp.mean(values, axis=-1, keepdims=True)
    spread = jnp.mean(center * center, axis=-1, keepdims=True)
    return center * lax.rsqrt(spread + 1e-05) * gain


def block_kernel(
    lons, lats,
    x_hbm, g1_hbm, wqkv_hbm, wproj_hbm, bias_hbm, g2_hbm, w1_hbm, w2t_hbm,
    out_hbm,
    xin, raw, lin, blo, bhi, frow, xlo, xhi, mixs, xqs, rlo, rhi, orow, stage,
    g1, g2, wqkv, wproj, w1, w2t,
    load_sem, own_sem, send_sem, recv_sem, out_sem,
):
    lon = lax.axis_index("lon")
    lat = lax.axis_index("lat")
    east = lax.rem(lon + 1, lons)
    west = lax.rem(lon + lons - 1, lons)
    south = lax.rem(lat + 1, lats)
    north = lax.rem(lat + lats - 1, lats)

    barrier = pltpu.get_barrier_semaphore()
    for a, b in ((west, lat), (east, lat), (lon, south), (west, south), (east, south), (lon, north)):
        pl.semaphore_signal(barrier, inc=1, device_id={"lon": a, "lat": b}, device_id_type=MESH)

    loads = [
        pltpu.make_async_copy(src, dst, load_sem.at[i])
        for i, (src, dst) in enumerate(
            (
                (bias_hbm, raw), (g1_hbm, g1), (wqkv_hbm, wqkv), (wproj_hbm, wproj),
                (g2_hbm, g2), (w1_hbm, w1), (w2t_hbm, w2t),
            )
        )
    ]
    own = [
        pltpu.make_async_copy(x_hbm.at[3:12, 0:9], xin.at[0, 0:9, 9:18], own_sem.at[0]),
        pltpu.make_async_copy(x_hbm.at[3:12, 9:18], xin.at[1, 0:9, 0:9], own_sem.at[1]),
    ]
    for copy in own + loads:
        copy.start()

    def remote(i, src, dst, a, b):
        return pltpu.make_async_remote_copy(
            src_ref=src, dst_ref=dst, send_sem=send_sem.at[i], recv_sem=recv_sem.at[i],
            device_id={"lon": a, "lat": b}, device_id_type=MESH,
        )

    halo = [
        remote(0, x_hbm.at[3:12, 0:9], xin.at[1, 0:9, 9:18], west, lat),
        remote(1, x_hbm.at[3:12, 9:18], xin.at[0, 0:9, 0:9], east, lat),
        remote(2, x_hbm.at[0:3, 0:9], xin.at[1, 9:12, 9:18], west, north),
        remote(3, x_hbm.at[0:3, 9:18], xin.at[0, 9:12, 0:9], east, north),
        remote(4, x_hbm.at[0:3, 0:9], xin.at[0, 9:12, 9:18], lon, north),
        remote(5, x_hbm.at[0:3, 9:18], xin.at[1, 9:12, 0:9], lon, north),
    ]
    give_back = remote(6, stage.at[9:12], out_hbm.at[0:3], lon, south)

    pl.semaphore_wait(barrier, 6)
    for copy in halo:
        copy.start()

    loads[0].wait()

    def linear(rh, carry):
        base = pl.multiple_of(rh * 324, 4)
        for t in range(162):
            lin[pl.ds(base + 2 * t, 2), :] = raw[rh, :, 128 * t : 128 * t + 128]
        return carry

    lax.fori_loop(0, 12, linear, 0)

    lanes = lax.broadcasted_iota(jnp.int32, (72, 128), 1)
    place = lax.broadcasted_iota(jnp.int32, (72, 128), 0)
    step = lax.rem(place, 6)
    level_q = step // 3
    last = jnp.where(lat == lats - 1, NEG, 0.0).astype(F32)

    def key_level(key):
        return key // 72

    def key_edge(key):
        return lax.rem(key // 12, 6) // 3

    edge_rows = place >= 36

    def penalty(key, odd, zwin):
        row_q = lax.rem(2 * step + odd, 6) // 3
        pen = jnp.where(jnp.logical_and(edge_rows, row_q != key_edge(key)), last, 0.0)
        if zwin:
            pen = pen + jnp.where(level_q != key_level(key), NEG, 0.0)
        return pen

    for zwin in range(2):
        for odd in range(2):
            pen_lo = penalty(lanes, odd, zwin)
            pen_hi = penalty(lanes + 128, odd, zwin)
            for wc in range(12):
                c = 12 * odd + wc
                start = (9 * (c // 8) + c % 8) * 2 + zwin
                this = lin[pl.ds(start, 72, stride=54), :]
                following = lin[pl.ds(start + 2, 72, stride=54), :]
                turn = 16 * (c % 8)
                if turn:
                    this = pltpu.roll(this, 128 - turn, 1)
                    following = pltpu.roll(following, 128 - turn, 1)
                low = jnp.where(lanes < 128 - turn, this, following)
                dest = (zwin * 2 + wc // 6) * 864 + 6 * odd + wc % 6
                blo[pl.ds(dest, 72, stride=12), :] = low + pen_lo
                bhi[pl.ds(dest, 72, stride=12), :] = following + pen_hi

    for copy in loads[1:]:
        copy.wait()
    for copy in own:
        copy.wait()
    for copy in halo:
        copy.wait()

    lane36 = lax.broadcasted_iota(jnp.int32, (36, 128), 1)
    lane18 = lax.broadcasted_iota(jnp.int32, (18, 128), 1)

    def prepare(rwin):
        for ew in range(2):
            tile = xin[ew, 6 * rwin : 6 * rwin + 6].astype(F32)
            frow[pl.ds((ew * 2 + rwin) * 432, 432), :] = tile.reshape(432, 128)
            for zwin in range(2):
                for lev in range(2):
                    base = (ew * 2 + rwin) * 432 + LEVEL[zwin][lev]
                    t0 = frow[pl.ds(base, 36, stride=12), :]
                    t1 = frow[pl.ds(base + 4, 36, stride=12), :]
                    t2 = frow[pl.ds(base + 8, 36, stride=12), :]
                    r1 = pltpu.roll(t1, 64, 1)
                    r2 = pltpu.roll(t2, 64, 1)
                    dest = ((rwin * 2 + zwin) * 2 + ew) * TOK + 72 * lev
                    xlo[pl.ds(dest, 36, stride=2), :] = t0
                    xhi[pl.ds(dest, 36, stride=2), :] = t1
                    xlo[pl.ds(dest + 1, 36, stride=2), :] = jnp.where(lane36 < 64, r1, r2)
                    xhi[pl.ds(dest + 1, 36, stride=2), :] = r2

    sel_k = lax.broadcasted_iota(jnp.int32, (HALF, TOK), 0)
    sel_i = lax.broadcasted_iota(jnp.int32, (HALF, TOK), 1)
    head_of = lax.broadcasted_iota(jnp.int32, (HALF, CH), 1) // HD
    scale = HD ** (-0.5)

    def attend(rwin, zwin, ew):
        win = (rwin * 2 + zwin) * 2 + ew
        half = 1 - ew
        rows = pl.ds(pl.multiple_of(win * TOK, 8), TOK)
        x = jnp.concatenate([xlo[rows, :], xhi[rows, :][:, : CH - 128]], axis=1)
        normed = layer_norm(x, g1[...]).astype(BF16)
        kv = dot(normed, wqkv[:, CH:]).astype(BF16)
        select = jnp.where(sel_i == sel_k + 6 * (sel_k // 6) + 6 * half, 1.0, 0.0).astype(BF16)
        query = dot(dot(select, normed).astype(BF16), wqkv[:, :CH]).astype(BF16).astype(F32)
        stacked = jnp.concatenate(
            [jnp.where(head_of == h, query, 0.0) for h in range(HEADS)], axis=0
        ).astype(BF16)
        scores = dot_nt(stacked, kv[:, :CH]) * scale
        brow = pl.ds(pl.multiple_of(((zwin * 2 + half) * 2 + rwin) * 432, 8), 432)
        scores = scores + jnp.concatenate([blo[brow, :], bhi[brow, :][:, :16]], axis=1)
        top = jnp.max(scores, axis=-1, keepdims=True)
        probs = jnp.exp(scores - top)
        total = jnp.sum(probs, axis=-1, keepdims=True)
        heads = dot(probs.astype(BF16), kv[:, CH:]) / total
        mixed = heads[:HALF]
        for h in range(1, HEADS):
            mixed = jnp.where(head_of == h, heads[h * HALF : (h + 1) * HALF], mixed)
        local = pl.ds(pl.multiple_of((zwin * 2 + ew) * HALF, 8), HALF)
        mixs[local, :] = mixed
        xqs[local, :] = dot(select, x.astype(BF16))

    def attend_all(rwin):
        def body(zwin, carry):
            attend(rwin, zwin, 0)
            attend(rwin, zwin, 1)
            return carry

        lax.fori_loop(0, 2, body, 0)

    def finish(rwin):
        attn = dot(mixs[...].astype(BF16), wproj[...]).astype(BF16).astype(F32)
        resid = (xqs[...] + attn).astype(BF16).astype(F32)
        normed = layer_norm(resid, g2[...]).astype(BF16)
        hidden = jax.nn.gelu(dot(normed, w1[...])).astype(BF16)
        result = resid + dot_nt(hidden, w2t[...])
        rlo[...] = result[:, :128]
        rhi[:, : CH - 128] = result[:, 128:]
        for zwin in range(2):
            for ew in range(2):
                for lev in range(2):
                    base = (zwin * 2 + ew) * HALF + 36 * lev
                    even_lo = rlo[pl.ds(base, 18, stride=2), :]
                    even_hi = rhi[pl.ds(base, 18, stride=2), :]
                    odd_lo = pltpu.roll(rlo[pl.ds(base + 1, 18, stride=2), :], 64, 1)
                    odd_hi = pltpu.roll(rhi[pl.ds(base + 1, 18, stride=2), :], 64, 1)
                    dest = (ew * 12 + 6 * rwin) * 36 + LEVEL[zwin][lev]
                    orow[pl.ds(dest, 18, stride=12), :] = even_lo
                    orow[pl.ds(dest + 4, 18, stride=12), :] = jnp.where(lane18 < 64, even_hi, odd_lo)
                    orow[pl.ds(dest + 8, 18, stride=12), :] = jnp.where(lane18 < 64, odd_lo, odd_hi)
        for ew in range(2):
            tile = orow[pl.ds((ew * 12 + 6 * rwin) * 36, 216), :].reshape(6, 9, 4, 128)
            stage[6 * rwin : 6 * rwin + 6, 9 * ew : 9 * ew + 9] = tile.astype(BF16)

    prepare(0)
    prepare(1)
    attend_all(1)
    finish(1)
    give_back.start()
    attend_all(0)
    finish(0)
    put = pltpu.make_async_copy(stage.at[0:9], out_hbm.at[3:12], out_sem)
    put.start()
    give_back.wait()
    put.wait()


def shards(field_in, g1, wqkv, wproj, bias, g2, w1, w2):
    lons, lats = lax.axis_size("lon"), lax.axis_size("lat")
    x = field_in.reshape(4, 12, 18, 128).transpose(1, 2, 0, 3)
    flat = bias.transpose(0, 2, 1, 3).reshape(12, 2, 20736)
    hbm = pl.BlockSpec(memory_space=pltpu.MemorySpace.HBM)
    out = pl.pallas_call(
        functools.partial(block_kernel, lons, lats),
        out_shape=jax.ShapeDtypeStruct((12, 18, 4, 128), BF16),
        in_specs=[hbm] * 8,
        out_specs=hbm,
        scratch_shapes=[
            pltpu.VMEM((2, 12, 18, 4, 128), BF16),
            pltpu.VMEM((12, 2, 20736), F32),
            pltpu.VMEM((3888, 128), F32),
            pltpu.VMEM((3456, 128), F32),
            pltpu.VMEM((3456, 128), F32),
            pltpu.VMEM((1728, 128), F32),
            pltpu.VMEM((1152, 128), F32),
            pltpu.VMEM((1152, 128), F32),
            pltpu.VMEM((288, CH), F32),
            pltpu.VMEM((288, CH), F32),
            pltpu.VMEM((288, 128), F32),
            pltpu.VMEM((288, 128), F32),
            pltpu.VMEM((864, 128), F32),
            pltpu.VMEM((12, 18, 4, 128), BF16),
            pltpu.VMEM((CH,), F32),
            pltpu.VMEM((CH,), F32),
            pltpu.VMEM((CH, 3 * CH), BF16),
            pltpu.VMEM((CH, CH), BF16),
            pltpu.VMEM((CH, 768), BF16),
            pltpu.VMEM((CH, 768), BF16),
            pltpu.SemaphoreType.DMA((7,)),
            pltpu.SemaphoreType.DMA((2,)),
            pltpu.SemaphoreType.DMA((7,)),
            pltpu.SemaphoreType.DMA((7,)),
            pltpu.SemaphoreType.DMA,
        ],
        compiler_params=pltpu.CompilerParams(
            collective_id=0, has_side_effects=True, vmem_limit_bytes=60 * 1024 * 1024
        ),
        name="swin_block",
    )(x, g1, wqkv, wproj, flat, g2, w1, w2.T)
    return out.transpose(2, 0, 1, 3).reshape(4, 12, 12 * CH)


def solution(mesh):
    in_specs = (P(None, "lat", "lon"), P(), P(), P(), P("lat", None, None, None), P(), P(), P())
    return jax.shard_map(
        shards, mesh=mesh, in_specs=in_specs, out_specs=P(None, "lat", "lon"), check_vma=False
    )
```

time: 73.1 us -> 32.3 us (0.44)
  the two profiles are of different devices: /device:TPU:8 before, /device:TPU:14 now
where the time goes in v1:
time: 32.3 us; the launch traced here: 32.1 us
  Pallas kernels  30.4 us (94%)
  local copies, waits for them, and re-layouts  1.7 us (5%)
    pallas_call x1, Pallas kernels, shards(): pl.pallas_call(functools.partial(block_kernel, lons, lats), out_shape=jax...  30.4 us
    unnamed x1, local copies, waits for them, and re-layouts  1.7 us

profile of v1, /device:TPU:14, one launch (start us, length us, event | category | flops | bytes accessed | tf_op | source)
XLA Modules:
  0.0 32.1 jit_solution(4568185789328207941)
XLA Ops:
  0.0 30.4 %swin_block.1 = bf16[12,18,4,128]{3,2,1,0:T(4,128)(2,1)} custom-call(bf16[12,18,4,128]{3,2,1,0:T(4,128)(2,1)} %bitcast.13, f32[192]{0:T(256)} %g1_hbm.1, bf16[192,576]{1,0:T(8,128)(2,1)} %wqkv_hbm.1, bf16[192,192]{1,0:T(8,128)(2,1)} %wproj_hbm.1, f32[12,2,20736]{2,1,0:T(2,128)} %bitcast.10, f32[192]{0:T(256)} %g2_hbm.1, bf16[192,768]{1,0:T(8,128)(2,1)} %w1_hbm.1, ...), custom_call_target="tpu_custom_call" | custom-call | tf_op jit(solution)/shard_map/swin_block/pallas_call | solution.py:249
  30.4 1.7 %copy.10 = bf16[4,12,2304]{2,0,1:T(4,128)(2,1)} copy(bf16[4,12,2304]{2,0,1:T(4,128)(2,1)} %bitcast.11) | data formatting | bytes 442368

commit v2 on v1

--- a/solution.py
+++ b/solution.py
@@ -36,10 +36,10 @@
 def block_kernel(
     lons, lats,
     x_hbm, g1_hbm, wqkv_hbm, wproj_hbm, bias_hbm, g2_hbm, w1_hbm, w2t_hbm,
-    out_hbm,
-    xin, raw, lin, blo, bhi, frow, xlo, xhi, mixs, xqs, rlo, rhi, orow, stage,
+    out,
+    xin, raw, lin, blo, bhi, frow, xlo, xhi, mixs, xqs, rlo, rhi, orow, back,
     g1, g2, wqkv, wproj, w1, w2t,
-    load_sem, own_sem, send_sem, recv_sem, out_sem,
+    load_sem, own_sem, send_sem, recv_sem,
 ):
     lon = lax.axis_index("lon")
     lat = lax.axis_index("lat")
@@ -75,14 +75,20 @@
         )
 
     halo = [
-        remote(0, x_hbm.at[3:12, 0:9], xin.at[1, 0:9, 9:18], west, lat),
-        remote(1, x_hbm.at[3:12, 9:18], xin.at[0, 0:9, 0:9], east, lat),
-        remote(2, x_hbm.at[0:3, 0:9], xin.at[1, 9:12, 9:18], west, north),
-        remote(3, x_hbm.at[0:3, 9:18], xin.at[0, 9:12, 0:9], east, north),
-        remote(4, x_hbm.at[0:3, 0:9], xin.at[0, 9:12, 9:18], lon, north),
-        remote(5, x_hbm.at[0:3, 9:18], xin.at[1, 9:12, 0:9], lon, north),
-    ]
-    give_back = remote(6, stage.at[9:12], out_hbm.at[0:3], lon, south)
+        remote(0, x_hbm.at[9:12, 9:18], xin.at[0, 6:9, 0:9], east, lat),
+        remote(1, x_hbm.at[0:3, 9:18], xin.at[0, 9:12, 0:9], east, north),
+        remote(2, x_hbm.at[3:9, 9:18], xin.at[0, 0:6, 0:9], east, lat),
+        remote(3, x_hbm.at[3:9, 0:9], xin.at[1, 0:6, 9:18], west, lat),
+        remote(4, x_hbm.at[9:12, 0:9], xin.at[1, 6:9, 9:18], west, lat),
+        remote(5, x_hbm.at[0:3, 0:9], xin.at[1, 9:12, 9:18], west, north),
+        remote(6, x_hbm.at[0:3, 9:18], xin.at[1, 9:12, 0:9], lon, north),
+        remote(7, x_hbm.at[0:3, 0:9], xin.at[0, 9:12, 9:18], lon, north),
+    ]
+    needs = {(0, 1): (3,), (1, 1): (4, 5, 6), (1, 0): (0, 1, 7), (0, 0): (2,)}
+    give_back = [
+        remote(8, back.at[:, 0:9], out.at[0:3, 0:9], lon, south),
+        remote(9, back.at[:, 9:18], out.at[0:3, 9:18], lon, south),
+    ]
 
     pl.semaphore_wait(barrier, 6)
     for copy in halo:
@@ -141,29 +147,26 @@
         copy.wait()
     for copy in own:
         copy.wait()
-    for copy in halo:
-        copy.wait()
 
     lane36 = lax.broadcasted_iota(jnp.int32, (36, 128), 1)
     lane18 = lax.broadcasted_iota(jnp.int32, (18, 128), 1)
 
-    def prepare(rwin):
-        for ew in range(2):
-            tile = xin[ew, 6 * rwin : 6 * rwin + 6].astype(F32)
-            frow[pl.ds((ew * 2 + rwin) * 432, 432), :] = tile.reshape(432, 128)
-            for zwin in range(2):
-                for lev in range(2):
-                    base = (ew * 2 + rwin) * 432 + LEVEL[zwin][lev]
-                    t0 = frow[pl.ds(base, 36, stride=12), :]
-                    t1 = frow[pl.ds(base + 4, 36, stride=12), :]
-                    t2 = frow[pl.ds(base + 8, 36, stride=12), :]
-                    r1 = pltpu.roll(t1, 64, 1)
-                    r2 = pltpu.roll(t2, 64, 1)
-                    dest = ((rwin * 2 + zwin) * 2 + ew) * TOK + 72 * lev
-                    xlo[pl.ds(dest, 36, stride=2), :] = t0
-                    xhi[pl.ds(dest, 36, stride=2), :] = t1
-                    xlo[pl.ds(dest + 1, 36, stride=2), :] = jnp.where(lane36 < 64, r1, r2)
-                    xhi[pl.ds(dest + 1, 36, stride=2), :] = r2
+    def prepare(rwin, ew):
+        tile = xin[ew, 6 * rwin : 6 * rwin + 6].astype(F32)
+        frow[pl.ds((ew * 2 + rwin) * 432, 432), :] = tile.reshape(432, 128)
+        for zwin in range(2):
+            for lev in range(2):
+                base = (ew * 2 + rwin) * 432 + LEVEL[zwin][lev]
+                t0 = frow[pl.ds(base, 36, stride=12), :]
+                t1 = frow[pl.ds(base + 4, 36, stride=12), :]
+                t2 = frow[pl.ds(base + 8, 36, stride=12), :]
+                r1 = pltpu.roll(t1, 64, 1)
+                r2 = pltpu.roll(t2, 64, 1)
+                dest = ((rwin * 2 + zwin) * 2 + ew) * TOK + 72 * lev
+                xlo[pl.ds(dest, 36, stride=2), :] = t0
+                xhi[pl.ds(dest, 36, stride=2), :] = t1
+                xlo[pl.ds(dest + 1, 36, stride=2), :] = jnp.where(lane36 < 64, r1, r2)
+                xhi[pl.ds(dest + 1, 36, stride=2), :] = r2
 
     sel_k = lax.broadcasted_iota(jnp.int32, (HALF, TOK), 0)
     sel_i = lax.broadcasted_iota(jnp.int32, (HALF, TOK), 1)
@@ -173,7 +176,7 @@
     def attend(rwin, zwin, ew):
         win = (rwin * 2 + zwin) * 2 + ew
         half = 1 - ew
-        rows = pl.ds(pl.multiple_of(win * TOK, 8), TOK)
+        rows = pl.ds(win * TOK, TOK)
         x = jnp.concatenate([xlo[rows, :], xhi[rows, :][:, : CH - 128]], axis=1)
         normed = layer_norm(x, g1[...]).astype(BF16)
         kv = dot(normed, wqkv[:, CH:]).astype(BF16)
@@ -183,62 +186,59 @@
             [jnp.where(head_of == h, query, 0.0) for h in range(HEADS)], axis=0
         ).astype(BF16)
         scores = dot_nt(stacked, kv[:, :CH]) * scale
-        brow = pl.ds(pl.multiple_of(((zwin * 2 + half) * 2 + rwin) * 432, 8), 432)
+        brow = pl.ds(((zwin * 2 + half) * 2 + rwin) * 432, 432)
         scores = scores + jnp.concatenate([blo[brow, :], bhi[brow, :][:, :16]], axis=1)
         top = jnp.max(scores, axis=-1, keepdims=True)
         probs = jnp.exp(scores - top)
         total = jnp.sum(probs, axis=-1, keepdims=True)
-        heads = dot(probs.astype(BF16), kv[:, CH:]) / total
+        heads = dot(probs.astype(BF16), kv[:, CH:]) * (1.0 / total)
         mixed = heads[:HALF]
         for h in range(1, HEADS):
             mixed = jnp.where(head_of == h, heads[h * HALF : (h + 1) * HALF], mixed)
-        local = pl.ds(pl.multiple_of((zwin * 2 + ew) * HALF, 8), HALF)
+        local = pl.ds((ew * 2 + zwin) * HALF, HALF)
         mixs[local, :] = mixed
         xqs[local, :] = dot(select, x.astype(BF16))
 
-    def attend_all(rwin):
-        def body(zwin, carry):
-            attend(rwin, zwin, 0)
-            attend(rwin, zwin, 1)
-            return carry
-
-        lax.fori_loop(0, 2, body, 0)
-
-    def finish(rwin):
-        attn = dot(mixs[...].astype(BF16), wproj[...]).astype(BF16).astype(F32)
-        resid = (xqs[...] + attn).astype(BF16).astype(F32)
+    def finish(rwin, ew):
+        group = pl.ds(ew * TOK, TOK)
+        attn = dot(mixs[group, :].astype(BF16), wproj[...]).astype(BF16).astype(F32)
+        resid = (xqs[group, :] + attn).astype(BF16).astype(F32)
         normed = layer_norm(resid, g2[...]).astype(BF16)
         hidden = jax.nn.gelu(dot(normed, w1[...])).astype(BF16)
         result = resid + dot_nt(hidden, w2t[...])
-        rlo[...] = result[:, :128]
-        rhi[:, : CH - 128] = result[:, 128:]
+        rlo[group, :] = result[:, :128]
+        rhi[group, : CH - 128] = result[:, 128:]
         for zwin in range(2):
-            for ew in range(2):
-                for lev in range(2):
-                    base = (zwin * 2 + ew) * HALF + 36 * lev
-                    even_lo = rlo[pl.ds(base, 18, stride=2), :]
-                    even_hi = rhi[pl.ds(base, 18, stride=2), :]
-                    odd_lo = pltpu.roll(rlo[pl.ds(base + 1, 18, stride=2), :], 64, 1)
-                    odd_hi = pltpu.roll(rhi[pl.ds(base + 1, 18, stride=2), :], 64, 1)
-                    dest = (ew * 12 + 6 * rwin) * 36 + LEVEL[zwin][lev]
-                    orow[pl.ds(dest, 18, stride=12), :] = even_lo
-                    orow[pl.ds(dest + 4, 18, stride=12), :] = jnp.where(lane18 < 64, even_hi, odd_lo)
-                    orow[pl.ds(dest + 8, 18, stride=12), :] = jnp.where(lane18 < 64, odd_lo, odd_hi)
-        for ew in range(2):
-            tile = orow[pl.ds((ew * 12 + 6 * rwin) * 36, 216), :].reshape(6, 9, 4, 128)
-            stage[6 * rwin : 6 * rwin + 6, 9 * ew : 9 * ew + 9] = tile.astype(BF16)
-
-    prepare(0)
-    prepare(1)
-    attend_all(1)
-    finish(1)
-    give_back.start()
-    attend_all(0)
-    finish(0)
-    put = pltpu.make_async_copy(stage.at[0:9], out_hbm.at[3:12], out_sem)
-    put.start()
-    give_back.wait()
-    put.wait()
+            for lev in range(2):
+                base = (ew * 2 + zwin) * HALF + 36 * lev
+                even_lo = rlo[pl.ds(base, 18, stride=2), :]
+                even_hi = rhi[pl.ds(base, 18, stride=2), :]
+                odd_lo = pltpu.roll(rlo[pl.ds(base + 1, 18, stride=2), :], 64, 1)
+                odd_hi = pltpu.roll(rhi[pl.ds(base + 1, 18, stride=2), :], 64, 1)
+                dest = (ew * 12 + 6 * rwin) * 36 + LEVEL[zwin][lev]
+                orow[pl.ds(dest, 18, stride=12), :] = even_lo
+                orow[pl.ds(dest + 4, 18, stride=12), :] = jnp.where(lane18 < 64, even_hi, odd_lo)
+                orow[pl.ds(dest + 8, 18, stride=12), :] = jnp.where(lane18 < 64, odd_lo, odd_hi)
+        tile = orow[pl.ds((ew * 12 + 6 * rwin) * 36, 216), :].reshape(6, 9, 4, 128).astype(BF16)
+        columns = pl.ds(9 * ew, 9)
+        if rwin == 0:
+            out[3:9, columns] = tile
+        else:
+            out[9:12, columns] = tile[:3]
+            back[:, columns] = tile[3:]
+            give_back[ew].start()
+
+    for rwin, ew in ((0, 1), (1, 1), (1, 0), (0, 0)):
+        for i in needs[rwin, ew]:
+            halo[i].wait_recv()
+        prepare(rwin, ew)
+        attend(rwin, 0, ew)
+        attend(rwin, 1, ew)
+        finish(rwin, ew)
+    for copy in halo:
+        copy.wait_send()
+    for copy in give_back:
+        copy.wait()
 
 
 def shards(field_in, g1, wqkv, wproj, bias, g2, w1, w2):
@@ -246,11 +246,11 @@
     x = field_in.reshape(4, 12, 18, 128).transpose(1, 2, 0, 3)
     flat = bias.transpose(0, 2, 1, 3).reshape(12, 2, 20736)
     hbm = pl.BlockSpec(memory_space=pltpu.MemorySpace.HBM)
-    out = pl.pallas_call(
+    result = pl.pallas_call(
         functools.partial(block_kernel, lons, lats),
-        out_shape=jax.ShapeDtypeStruct((12, 18, 4, 128), BF16),
+        out_shape=pltpu.VMEM((12, 18, 4, 128), BF16),
         in_specs=[hbm] * 8,
-        out_specs=hbm,
+        out_specs=pl.BlockSpec(memory_space=pltpu.VMEM),
         scratch_shapes=[
             pltpu.VMEM((2, 12, 18, 4, 128), BF16),
             pltpu.VMEM((12, 2, 20736), F32),
@@ -265,7 +265,7 @@
             pltpu.VMEM((288, 128), F32),
             pltpu.VMEM((288, 128), F32),
             pltpu.VMEM((864, 128), F32),
-            pltpu.VMEM((12, 18, 4, 128), BF16),
+            pltpu.VMEM((3, 18, 4, 128), BF16),
             pltpu.VMEM((CH,), F32),
             pltpu.VMEM((CH,), F32),
             pltpu.VMEM((CH, 3 * CH), BF16),
@@ -274,16 +274,15 @@
             pltpu.VMEM((CH, 768), BF16),
             pltpu.SemaphoreType.DMA((7,)),
             pltpu.SemaphoreType.DMA((2,)),
-            pltpu.SemaphoreType.DMA((7,)),
-            pltpu.SemaphoreType.DMA((7,)),
-            pltpu.SemaphoreType.DMA,
+            pltpu.SemaphoreType.DMA((10,)),
+            pltpu.SemaphoreType.DMA((10,)),
         ],
         compiler_params=pltpu.CompilerParams(
             collective_id=0, has_side_effects=True, vmem_limit_bytes=60 * 1024 * 1024
         ),
         name="swin_block",
     )(x, g1, wqkv, wproj, flat, g2, w1, w2.T)
-    return out.transpose(2, 0, 1, 3).reshape(4, 12, 12 * CH)
+    return result.transpose(2, 0, 1, 3).reshape(4, 12, 12 * CH)
 
 
 def solution(mesh):

time: 32.3 us -> 30.6 us (0.947)
  the two profiles are of different devices: /device:TPU:14 before, /device:TPU:8 now
where the time goes in v2:
time: 30.6 us; the launch traced here: 30.5 us
  Pallas kernels  29.8 us (97%)
  local copies, waits for them, and re-layouts  0.69 us (2%)
    pallas_call x1, Pallas kernels, shards(): pl.pallas_call(functools.partial(block_kernel, lons, lats), out_shape=plt...  29.8 us
    unnamed x1, local copies, waits for them, and re-layouts  0.69 us

profile of v2, /device:TPU:8, one launch (start us, length us, event | category | flops | bytes accessed | tf_op | source)
XLA Modules:
  0.0 30.5 jit_solution(4739235815842567011)
XLA Ops:
  0.0 29.8 %swin_block.1 = bf16[12,18,4,128]{3,2,1,0:T(4,128)(2,1)S(1)} custom-call(bf16[12,18,4,128]{3,2,1,0:T(4,128)(2,1)} %bitcast.13, f32[192]{0:T(256)} %g1_hbm.1, bf16[192,576]{1,0:T(8,128)(2,1)} %wqkv_hbm.1, bf16[192,192]{1,0:T(8,128)(2,1)} %wproj_hbm.1, f32[12,2,20736]{2,1,0:T(2,128)} %bitcast.11, f32[192]{0:T(256)} %g2_hbm.1, bf16[192,768]{1,0:T(8,128)(2,1)} %w1_hbm.1, ...), custom_call_target="tpu_custom_call" | custom-call | tf_op jit(solution)/shard_map/swin_block/pallas_call | solution.py:249
  29.8 0.7 %copy.10 = bf16[4,12,2304]{2,0,1:T(4,128)(2,1)} copy(bf16[4,12,2304]{2,0,1:T(4,128)(2,1)S(1)} %bitcast.10) | data formatting | bytes 442368

commit v3 on v2

--- a/solution.py
+++ b/solution.py
@@ -39,7 +39,7 @@
     out,
     xin, raw, lin, blo, bhi, frow, xlo, xhi, mixs, xqs, rlo, rhi, orow, back,
     g1, g2, wqkv, wproj, w1, w2t,
-    load_sem, own_sem, send_sem, recv_sem,
+    load_sem, own_sem, send_sem, recv_sem, ready,
 ):
     lon = lax.axis_index("lon")
     lat = lax.axis_index("lat")
@@ -49,7 +49,7 @@
     north = lax.rem(lat + lats - 1, lats)
 
     barrier = pltpu.get_barrier_semaphore()
-    for a, b in ((west, lat), (east, lat), (lon, south), (west, south), (east, south), (lon, north)):
+    for a, b in ((west, lat), (lon, south), (west, south), (west, north)):
         pl.semaphore_signal(barrier, inc=1, device_id={"lon": a, "lat": b}, device_id_type=MESH)
 
     loads = [
@@ -90,9 +90,23 @@
         remote(9, back.at[:, 9:18], out.at[0:3, 9:18], lon, south),
     ]
 
-    pl.semaphore_wait(barrier, 6)
-    for copy in halo:
-        copy.start()
+    pl.semaphore_wait(barrier, 4)
+    for i, (a, b) in enumerate(((east, lat), (east, south), (lon, north))):
+        pl.semaphore_signal(ready.at[i], inc=1, device_id={"lon": a, "lat": b}, device_id_type=MESH)
+    for i in (0, 1, 2, 6, 7):
+        halo[i].start()
+
+    def westward():
+        pl.semaphore_wait(ready.at[0], 1)
+        pl.semaphore_wait(ready.at[1], 1)
+        for i in (3, 4, 5):
+            halo[i].start()
+
+    across = lax.rem(lon, 16) == 0
+
+    @pl.when(jnp.logical_not(across))
+    def _():
+        westward()
 
     loads[0].wait()
 
@@ -226,9 +240,14 @@
         else:
             out[9:12, columns] = tile[:3]
             back[:, columns] = tile[3:]
-            give_back[ew].start()
+            if ew == 0:
+                give_back[0].start()
 
     for rwin, ew in ((0, 1), (1, 1), (1, 0), (0, 0)):
+        if (rwin, ew) == (1, 0):
+            pl.when(across)(westward)
+            pl.semaphore_wait(ready.at[2], 1)
+            give_back[1].start()
         for i in needs[rwin, ew]:
             halo[i].wait_recv()
         prepare(rwin, ew)
@@ -276,6 +295,7 @@
             pltpu.SemaphoreType.DMA((2,)),
             pltpu.SemaphoreType.DMA((10,)),
             pltpu.SemaphoreType.DMA((10,)),
+            pltpu.SemaphoreType.REGULAR((3,)),
         ],
         compiler_params=pltpu.CompilerParams(
             collective_id=0, has_side_effects=True, vmem_limit_bytes=60 * 1024 * 1024

time: 30.6 us -> 26.6 us (0.87)
  Pallas kernels: 29.8 us -> 25.8 us
    pallas_call x1, Pallas kernels: 29.8 us -> 25.8 us  [shards(): pl.pallas_call(functools.partial(block_kernel, lons, lats), out_shape=plt...]
where the time goes in v3:
time: 26.6 us; the launch traced here: 26.5 us
  Pallas kernels  25.8 us (97%)
  local copies, waits for them, and re-layouts  0.69 us (3%)
    pallas_call x1, Pallas kernels, shards(): pl.pallas_call(functools.partial(block_kernel, lons, lats), out_shape=plt...  25.8 us
    unnamed x1, local copies, waits for them, and re-layouts  0.69 us

profile of v3, /device:TPU:8, one launch (start us, length us, event | category | flops | bytes accessed | tf_op | source)
XLA Modules:
  0.0 26.5 jit_solution(6096015419411448561)
XLA Ops:
  0.0 25.8 %swin_block.1 = bf16[12,18,4,128]{3,2,1,0:T(4,128)(2,1)S(1)} custom-call(bf16[12,18,4,128]{3,2,1,0:T(4,128)(2,1)} %bitcast.13, f32[192]{0:T(256)} %g1_hbm.1, bf16[192,576]{1,0:T(8,128)(2,1)} %wqkv_hbm.1, bf16[192,192]{1,0:T(8,128)(2,1)} %wproj_hbm.1, f32[12,2,20736]{2,1,0:T(2,128)} %bitcast.11, f32[192]{0:T(256)} %g2_hbm.1, bf16[192,768]{1,0:T(8,128)(2,1)} %w1_hbm.1, ...), custom_call_target="tpu_custom_call" | custom-call | tf_op jit(solution)/shard_map/swin_block/pallas_call | solution.py:268
  25.8 0.7 %copy.10 = bf16[4,12,2304]{2,0,1:T(4,128)(2,1)} copy(bf16[4,12,2304]{2,0,1:T(4,128)(2,1)S(1)} %bitcast.10) | data formatting | bytes 442368

commit v4 on v3

--- a/solution.py
+++ b/solution.py
@@ -49,7 +49,7 @@
     north = lax.rem(lat + lats - 1, lats)
 
     barrier = pltpu.get_barrier_semaphore()
-    for a, b in ((west, lat), (lon, south), (west, south), (west, north)):
+    for a, b in ((west, lat), (lon, north), (west, south), (west, north)):
         pl.semaphore_signal(barrier, inc=1, device_id={"lon": a, "lat": b}, device_id_type=MESH)
 
     loads = [
@@ -84,16 +84,17 @@
         remote(6, x_hbm.at[0:3, 9:18], xin.at[1, 9:12, 0:9], lon, north),
         remote(7, x_hbm.at[0:3, 0:9], xin.at[0, 9:12, 9:18], lon, north),
     ]
-    needs = {(0, 1): (3,), (1, 1): (4, 5, 6), (1, 0): (0, 1, 7), (0, 0): (2,)}
-    give_back = [
-        remote(8, back.at[:, 0:9], out.at[0:3, 0:9], lon, south),
-        remote(9, back.at[:, 9:18], out.at[0:3, 9:18], lon, south),
-    ]
+    needs = (((2,), (0, 1, 7)), ((3,), (4, 5, 6)))
+
+    def give_back(ew):
+        columns = pl.ds(9 * ew, 9)
+        return remote(8 + ew, back.at[:, columns], out.at[0:3, columns], lon, south)
+
 
     pl.semaphore_wait(barrier, 4)
-    for i, (a, b) in enumerate(((east, lat), (east, south), (lon, north))):
+    for i, (a, b) in enumerate(((east, lat), (east, south), (lon, south))):
         pl.semaphore_signal(ready.at[i], inc=1, device_id={"lon": a, "lat": b}, device_id_type=MESH)
-    for i in (0, 1, 2, 6, 7):
+    for i in (1, 0, 2):
         halo[i].start()
 
     def westward():
@@ -101,12 +102,6 @@
         pl.semaphore_wait(ready.at[1], 1)
         for i in (3, 4, 5):
             halo[i].start()
-
-    across = lax.rem(lon, 16) == 0
-
-    @pl.when(jnp.logical_not(across))
-    def _():
-        westward()
 
     loads[0].wait()
 
@@ -157,6 +152,15 @@
                 blo[pl.ds(dest, 72, stride=12), :] = low + pen_lo
                 bhi[pl.ds(dest, 72, stride=12), :] = following + pen_hi
 
+    pl.semaphore_wait(ready.at[2], 1)
+    for i in (6, 7):
+        halo[i].start()
+    across = lax.rem(lon, 16) == 0
+
+    @pl.when(jnp.logical_not(across))
+    def _():
+        westward()
+
     for copy in loads[1:]:
         copy.wait()
     for copy in own:
@@ -167,7 +171,7 @@
 
     def prepare(rwin, ew):
         tile = xin[ew, 6 * rwin : 6 * rwin + 6].astype(F32)
-        frow[pl.ds((ew * 2 + rwin) * 432, 432), :] = tile.reshape(432, 128)
+        frow[pl.ds(pl.multiple_of((ew * 2 + rwin) * 432, 8), 432), :] = tile.reshape(432, 128)
         for zwin in range(2):
             for lev in range(2):
                 base = (ew * 2 + rwin) * 432 + LEVEL[zwin][lev]
@@ -190,7 +194,7 @@
     def attend(rwin, zwin, ew):
         win = (rwin * 2 + zwin) * 2 + ew
         half = 1 - ew
-        rows = pl.ds(win * TOK, TOK)
+        rows = pl.ds(pl.multiple_of(win * TOK, 8), TOK)
         x = jnp.concatenate([xlo[rows, :], xhi[rows, :][:, : CH - 128]], axis=1)
         normed = layer_norm(x, g1[...]).astype(BF16)
         kv = dot(normed, wqkv[:, CH:]).astype(BF16)
@@ -200,7 +204,7 @@
             [jnp.where(head_of == h, query, 0.0) for h in range(HEADS)], axis=0
         ).astype(BF16)
         scores = dot_nt(stacked, kv[:, :CH]) * scale
-        brow = pl.ds(((zwin * 2 + half) * 2 + rwin) * 432, 432)
+        brow = pl.ds(pl.multiple_of(((zwin * 2 + half) * 2 + rwin) * 432, 8), 432)
         scores = scores + jnp.concatenate([blo[brow, :], bhi[brow, :][:, :16]], axis=1)
         top = jnp.max(scores, axis=-1, keepdims=True)
         probs = jnp.exp(scores - top)
@@ -209,12 +213,12 @@
         mixed = heads[:HALF]
         for h in range(1, HEADS):
             mixed = jnp.where(head_of == h, heads[h * HALF : (h + 1) * HALF], mixed)
-        local = pl.ds((ew * 2 + zwin) * HALF, HALF)
+        local = pl.ds(pl.multiple_of((ew * 2 + zwin) * HALF, 8), HALF)
         mixs[local, :] = mixed
         xqs[local, :] = dot(select, x.astype(BF16))
 
     def finish(rwin, ew):
-        group = pl.ds(ew * TOK, TOK)
+        group = pl.ds(pl.multiple_of(ew * TOK, 8), TOK)
         attn = dot(mixs[group, :].astype(BF16), wproj[...]).astype(BF16).astype(F32)
         resid = (xqs[group, :] + attn).astype(BF16).astype(F32)
         normed = layer_norm(resid, g2[...]).astype(BF16)
@@ -233,31 +237,38 @@
                 orow[pl.ds(dest, 18, stride=12), :] = even_lo
                 orow[pl.ds(dest + 4, 18, stride=12), :] = jnp.where(lane18 < 64, even_hi, odd_lo)
                 orow[pl.ds(dest + 8, 18, stride=12), :] = jnp.where(lane18 < 64, odd_lo, odd_hi)
-        tile = orow[pl.ds((ew * 12 + 6 * rwin) * 36, 216), :].reshape(6, 9, 4, 128).astype(BF16)
+        tile = orow[pl.ds(pl.multiple_of((ew * 12 + 6 * rwin) * 36, 8), 216), :].reshape(6, 9, 4, 128).astype(BF16)
         columns = pl.ds(9 * ew, 9)
         if rwin == 0:
             out[3:9, columns] = tile
         else:
             out[9:12, columns] = tile[:3]
             back[:, columns] = tile[3:]
-            if ew == 0:
-                give_back[0].start()
-
-    for rwin, ew in ((0, 1), (1, 1), (1, 0), (0, 0)):
-        if (rwin, ew) == (1, 0):
-            pl.when(across)(westward)
-            pl.semaphore_wait(ready.at[2], 1)
-            give_back[1].start()
-        for i in needs[rwin, ew]:
-            halo[i].wait_recv()
+            give_back(ew).start()
+
+    def group(rwin, ew):
+        for side in range(2):
+
+            @pl.when(ew == side)
+            def _(side=side):
+                for i in needs[side][rwin]:
+                    halo[i].wait_recv()
+
         prepare(rwin, ew)
         attend(rwin, 0, ew)
         attend(rwin, 1, ew)
         finish(rwin, ew)
+
+    early = jnp.where(across, 1, 0)
+    group(0, early)
+    group(1, early)
+    pl.when(across)(westward)
+    group(1, 1 - early)
+    group(0, 1 - early)
     for copy in halo:
         copy.wait_send()
-    for copy in give_back:
-        copy.wait()
+    for ew in range(2):
+        give_back(ew).wait()
 
 
 def shards(field_in, g1, wqkv, wproj, bias, g2, w1, w2):

time: 26.6 us -> 23.5 us (0.88)
  Pallas kernels: 25.8 us -> 22.7 us
    pallas_call x1, Pallas kernels: 25.8 us -> 22.7 us  [shards(): pl.pallas_call(functools.partial(block_kernel, lons, lats), out_shape=plt...]
where the time goes in v4:
time: 23.5 us; the launch traced here: 23.4 us
  Pallas kernels  22.7 us (97%)
  local copies, waits for them, and re-layouts  0.69 us (3%)
    pallas_call x1, Pallas kernels, shards(): pl.pallas_call(functools.partial(block_kernel, lons, lats), out_shape=plt...  22.7 us
    unnamed x1, local copies, waits for them, and re-layouts  0.69 us

profile of v4, /device:TPU:8, one launch (start us, length us, event | category | flops | bytes accessed | tf_op | source)
XLA Modules:
  0.0 23.4 jit_solution(2434674912021327609)
XLA Ops:
  0.0 22.7 %swin_block.1 = bf16[12,18,4,128]{3,2,1,0:T(4,128)(2,1)S(1)} custom-call(bf16[12,18,4,128]{3,2,1,0:T(4,128)(2,1)} %bitcast.13, f32[192]{0:T(256)} %g1_hbm.1, bf16[192,576]{1,0:T(8,128)(2,1)} %wqkv_hbm.1, bf16[192,192]{1,0:T(8,128)(2,1)} %wproj_hbm.1, f32[12,2,20736]{2,1,0:T(2,128)} %bitcast.11, f32[192]{0:T(256)} %g2_hbm.1, bf16[192,768]{1,0:T(8,128)(2,1)} %w1_hbm.1, ...), custom_call_target="tpu_custom_call" | custom-call | tf_op jit(solution)/shard_map/swin_block/pallas_call | solution.py:279
  22.7 0.7 %copy.10 = bf16[4,12,2304]{2,0,1:T(4,128)(2,1)} copy(bf16[4,12,2304]{2,0,1:T(4,128)(2,1)S(1)} %bitcast.10) | data formatting | bytes 442368

commit v5 on v4

--- a/solution.py
+++ b/solution.py
@@ -17,6 +17,7 @@
 HALF = TOK // 2
 LEVEL = ((1, 2), (3, 0))
 NEG = -1000000000.0
+LOG2E = 1.4426950408889634
 
 
 def dot_nt(a, b):
@@ -37,7 +38,7 @@
     lons, lats,
     x_hbm, g1_hbm, wqkv_hbm, wproj_hbm, bias_hbm, g2_hbm, w1_hbm, w2t_hbm,
     out,
-    xin, raw, lin, blo, bhi, frow, xlo, xhi, mixs, xqs, rlo, rhi, orow, back,
+    xin, raw, lin, blo, bhi, fq, qlo, qhi, stack, qst, frow, xlo, xhi, mixs, rlo, rhi, orow, back,
     g1, g2, wqkv, wproj, w1, w2t,
     load_sem, own_sem, send_sem, recv_sem, ready,
 ):
@@ -84,7 +85,8 @@
         remote(6, x_hbm.at[0:3, 9:18], xin.at[1, 9:12, 0:9], lon, north),
         remote(7, x_hbm.at[0:3, 0:9], xin.at[0, 9:12, 9:18], lon, north),
     ]
-    needs = (((2,), (0, 1, 7)), ((3,), (4, 5, 6)))
+    query_needs = (((), (7,)), ((), (6,)))
+    key_needs = (((2,), (0, 1)), ((3,), (4, 5)))
 
     def give_back(ew):
         columns = pl.ds(9 * ew, 9)
@@ -149,8 +151,8 @@
                     following = pltpu.roll(following, 128 - turn, 1)
                 low = jnp.where(lanes < 128 - turn, this, following)
                 dest = (zwin * 2 + wc // 6) * 864 + 6 * odd + wc % 6
-                blo[pl.ds(dest, 72, stride=12), :] = low + pen_lo
-                bhi[pl.ds(dest, 72, stride=12), :] = following + pen_hi
+                blo[pl.ds(dest, 72, stride=12), :] = low * LOG2E + pen_lo
+                bhi[pl.ds(dest, 72, stride=12), :] = following * LOG2E + pen_hi
 
     pl.semaphore_wait(ready.at[2], 1)
     for i in (6, 7):
@@ -169,75 +171,89 @@
     lane36 = lax.broadcasted_iota(jnp.int32, (36, 128), 1)
     lane18 = lax.broadcasted_iota(jnp.int32, (18, 128), 1)
 
-    def prepare(rwin, ew):
+    head_of = lax.broadcasted_iota(jnp.int32, (HALF, CH), 1) // HD
+
+    def queries(rwin, ew):
+        own_tiles = pl.ds(9 - 9 * ew, 9)
+        tile = xin[ew, 6 * rwin : 6 * rwin + 6, own_tiles].astype(F32)
+        fq[rwin * 216 : rwin * 216 + 216, :] = tile.reshape(216, 128)
+        for zwin in range(2):
+            for lev in range(2):
+                base = rwin * 216 + LEVEL[zwin][lev]
+                t0 = fq[pl.ds(base, 18, stride=12), :]
+                t1 = fq[pl.ds(base + 4, 18, stride=12), :]
+                t2 = fq[pl.ds(base + 8, 18, stride=12), :]
+                r1 = pltpu.roll(t1, 64, 1)
+                r2 = pltpu.roll(t2, 64, 1)
+                dest = rwin * TOK + zwin * HALF + 36 * lev
+                qlo[pl.ds(dest, 18, stride=2), :] = t0
+                qhi[pl.ds(dest, 18, stride=2), :] = t1
+                qlo[pl.ds(dest + 1, 18, stride=2), :] = jnp.where(lane18 < 64, r1, r2)
+                qhi[pl.ds(dest + 1, 18, stride=2), :] = r2
+        normed = layer_norm(tokens(qlo, qhi, rwin * TOK, TOK), g1[...]).astype(BF16)
+        query = dot(normed, wqkv[:, :CH]) * (HD ** (-0.5) * LOG2E)
+        for zwin in range(2):
+            part = query[zwin * HALF : (zwin + 1) * HALF]
+            for h in range(HEADS):
+                stack[pl.ds(h * HALF, HALF), :] = jnp.where(head_of == h, part, 0.0)
+            qst[rwin, zwin] = stack[...].astype(BF16)
+
+    def tokens(low, high, start, size):
+        return jnp.concatenate([low[start : start + size, :], high[start : start + size, : CH - 128]], axis=1)
+
+    def attend(rwin, ew):
         tile = xin[ew, 6 * rwin : 6 * rwin + 6].astype(F32)
-        frow[pl.ds(pl.multiple_of((ew * 2 + rwin) * 432, 8), 432), :] = tile.reshape(432, 128)
+        frow[rwin * 432 : rwin * 432 + 432, :] = tile.reshape(432, 128)
         for zwin in range(2):
             for lev in range(2):
-                base = (ew * 2 + rwin) * 432 + LEVEL[zwin][lev]
+                base = rwin * 432 + LEVEL[zwin][lev]
                 t0 = frow[pl.ds(base, 36, stride=12), :]
                 t1 = frow[pl.ds(base + 4, 36, stride=12), :]
                 t2 = frow[pl.ds(base + 8, 36, stride=12), :]
                 r1 = pltpu.roll(t1, 64, 1)
                 r2 = pltpu.roll(t2, 64, 1)
-                dest = ((rwin * 2 + zwin) * 2 + ew) * TOK + 72 * lev
+                dest = (rwin * 2 + zwin) * TOK + 72 * lev
                 xlo[pl.ds(dest, 36, stride=2), :] = t0
                 xhi[pl.ds(dest, 36, stride=2), :] = t1
                 xlo[pl.ds(dest + 1, 36, stride=2), :] = jnp.where(lane36 < 64, r1, r2)
                 xhi[pl.ds(dest + 1, 36, stride=2), :] = r2
-
-    sel_k = lax.broadcasted_iota(jnp.int32, (HALF, TOK), 0)
-    sel_i = lax.broadcasted_iota(jnp.int32, (HALF, TOK), 1)
-    head_of = lax.broadcasted_iota(jnp.int32, (HALF, CH), 1) // HD
-    scale = HD ** (-0.5)
-
-    def attend(rwin, zwin, ew):
-        win = (rwin * 2 + zwin) * 2 + ew
-        half = 1 - ew
-        rows = pl.ds(pl.multiple_of(win * TOK, 8), TOK)
-        x = jnp.concatenate([xlo[rows, :], xhi[rows, :][:, : CH - 128]], axis=1)
-        normed = layer_norm(x, g1[...]).astype(BF16)
+        normed = layer_norm(tokens(xlo, xhi, rwin * 2 * TOK, 2 * TOK), g1[...]).astype(BF16)
         kv = dot(normed, wqkv[:, CH:]).astype(BF16)
-        select = jnp.where(sel_i == sel_k + 6 * (sel_k // 6) + 6 * half, 1.0, 0.0).astype(BF16)
-        query = dot(dot(select, normed).astype(BF16), wqkv[:, :CH]).astype(BF16).astype(F32)
-        stacked = jnp.concatenate(
-            [jnp.where(head_of == h, query, 0.0) for h in range(HEADS)], axis=0
-        ).astype(BF16)
-        scores = dot_nt(stacked, kv[:, :CH]) * scale
-        brow = pl.ds(pl.multiple_of(((zwin * 2 + half) * 2 + rwin) * 432, 8), 432)
-        scores = scores + jnp.concatenate([blo[brow, :], bhi[brow, :][:, :16]], axis=1)
-        top = jnp.max(scores, axis=-1, keepdims=True)
-        probs = jnp.exp(scores - top)
-        total = jnp.sum(probs, axis=-1, keepdims=True)
-        heads = dot(probs.astype(BF16), kv[:, CH:]) * (1.0 / total)
-        mixed = heads[:HALF]
-        for h in range(1, HEADS):
-            mixed = jnp.where(head_of == h, heads[h * HALF : (h + 1) * HALF], mixed)
-        local = pl.ds(pl.multiple_of((ew * 2 + zwin) * HALF, 8), HALF)
-        mixs[local, :] = mixed
-        xqs[local, :] = dot(select, x.astype(BF16))
+        for zwin in range(2):
+            mine = kv[zwin * TOK : (zwin + 1) * TOK]
+            scores = dot_nt(qst[rwin, zwin], mine[:, :CH])
+            brow = pl.ds(pl.multiple_of(((zwin * 2 + 1 - ew) * 2 + rwin) * 432, 8), 432)
+            scores = scores + jnp.concatenate([blo[brow, :], bhi[brow, :][:, :16]], axis=1)
+            top = jnp.max(scores, axis=-1, keepdims=True)
+            probs = jnp.exp2(scores - top)
+            total = jnp.sum(probs, axis=-1, keepdims=True)
+            heads = dot(probs.astype(BF16), mine[:, CH:])
+            mixed, norm = heads[:HALF], jnp.broadcast_to(total[:HALF], (HALF, CH))
+            for h in range(1, HEADS):
+                mixed = jnp.where(head_of == h, heads[h * HALF : (h + 1) * HALF], mixed)
+                norm = jnp.where(head_of == h, total[h * HALF : (h + 1) * HALF], norm)
+            mixs[rwin, zwin * HALF : (zwin + 1) * HALF, :] = mixed / norm
 
     def finish(rwin, ew):
-        group = pl.ds(pl.multiple_of(ew * TOK, 8), TOK)
-        attn = dot(mixs[group, :].astype(BF16), wproj[...]).astype(BF16).astype(F32)
-        resid = (xqs[group, :] + attn).astype(BF16).astype(F32)
+        attn = dot(mixs[rwin].astype(BF16), wproj[...]).astype(BF16).astype(F32)
+        resid = (tokens(qlo, qhi, rwin * TOK, TOK) + attn).astype(BF16).astype(F32)
         normed = layer_norm(resid, g2[...]).astype(BF16)
         hidden = jax.nn.gelu(dot(normed, w1[...])).astype(BF16)
         result = resid + dot_nt(hidden, w2t[...])
-        rlo[group, :] = result[:, :128]
-        rhi[group, : CH - 128] = result[:, 128:]
+        rlo[...] = result[:, :128]
+        rhi[:, : CH - 128] = result[:, 128:]
         for zwin in range(2):
             for lev in range(2):
-                base = (ew * 2 + zwin) * HALF + 36 * lev
+                base = zwin * HALF + 36 * lev
                 even_lo = rlo[pl.ds(base, 18, stride=2), :]
                 even_hi = rhi[pl.ds(base, 18, stride=2), :]
                 odd_lo = pltpu.roll(rlo[pl.ds(base + 1, 18, stride=2), :], 64, 1)
                 odd_hi = pltpu.roll(rhi[pl.ds(base + 1, 18, stride=2), :], 64, 1)
-                dest = (ew * 12 + 6 * rwin) * 36 + LEVEL[zwin][lev]
+                dest = LEVEL[zwin][lev]
                 orow[pl.ds(dest, 18, stride=12), :] = even_lo
                 orow[pl.ds(dest + 4, 18, stride=12), :] = jnp.where(lane18 < 64, even_hi, odd_lo)
                 orow[pl.ds(dest + 8, 18, stride=12), :] = jnp.where(lane18 < 64, odd_lo, odd_hi)
-        tile = orow[pl.ds(pl.multiple_of((ew * 12 + 6 * rwin) * 36, 8), 216), :].reshape(6, 9, 4, 128).astype(BF16)
+        tile = orow[...].reshape(6, 9, 4, 128).astype(BF16)
         columns = pl.ds(9 * ew, 9)
         if rwin == 0:
             out[3:9, columns] = tile
@@ -246,25 +262,30 @@
             back[:, columns] = tile[3:]
             give_back(ew).start()
 
-    def group(rwin, ew):
+    def arrive(which, rwin, ew):
         for side in range(2):
 
             @pl.when(ew == side)
             def _(side=side):
-                for i in needs[side][rwin]:
+                for i in which[side][rwin]:
                     halo[i].wait_recv()
 
-        prepare(rwin, ew)
-        attend(rwin, 0, ew)
-        attend(rwin, 1, ew)
-        finish(rwin, ew)
-
     early = jnp.where(across, 1, 0)
-    group(0, early)
-    group(1, early)
+    late = 1 - early
+    for rwin in range(2):
+        arrive(query_needs, rwin, early)
+        queries(rwin, early)
+        arrive(key_needs, rwin, early)
+        attend(rwin, early)
+        finish(rwin, early)
+    for rwin in (1, 0):
+        arrive(query_needs, rwin, late)
+        queries(rwin, late)
     pl.when(across)(westward)
-    group(1, 1 - early)
-    group(0, 1 - early)
+    for rwin in (1, 0):
+        arrive(key_needs, rwin, late)
+        attend(rwin, late)
+        finish(rwin, late)
     for copy in halo:
         copy.wait_send()
     for ew in range(2):
@@ -287,14 +308,18 @@
             pltpu.VMEM((3888, 128), F32),
             pltpu.VMEM((3456, 128), F32),
             pltpu.VMEM((3456, 128), F32),
-            pltpu.VMEM((1728, 128), F32),
-            pltpu.VMEM((1152, 128), F32),
-            pltpu.VMEM((1152, 128), F32),
-            pltpu.VMEM((288, CH), F32),
-            pltpu.VMEM((288, CH), F32),
+            pltpu.VMEM((432, 128), F32),
             pltpu.VMEM((288, 128), F32),
             pltpu.VMEM((288, 128), F32),
+            pltpu.VMEM((432, CH), F32),
+            pltpu.VMEM((2, 2, 432, CH), BF16),
             pltpu.VMEM((864, 128), F32),
+            pltpu.VMEM((576, 128), F32),
+            pltpu.VMEM((576, 128), F32),
+            pltpu.VMEM((2, TOK, CH), F32),
+            pltpu.VMEM((TOK, 128), F32),
+            pltpu.VMEM((TOK, 128), F32),
+            pltpu.VMEM((216, 128), F32),
             pltpu.VMEM((3, 18, 4, 128), BF16),
             pltpu.VMEM((CH,), F32),
             pltpu.VMEM((CH,), F32),

time: 23.5 us -> 23.2 us (0.987)
  Pallas kernels: 22.7 us -> 22.4 us
    pallas_call x1, Pallas kernels: 22.7 us -> 22.4 us  [shards(): pl.pallas_call(functools.partial(block_kernel, lons, lats), out_shape=plt...]
where the time goes in v5:
time: 23.2 us; the launch traced here: 23.1 us
  Pallas kernels  22.4 us (97%)
  local copies, waits for them, and re-layouts  0.69 us (3%)
    pallas_call x1, Pallas kernels, shards(): pl.pallas_call(functools.partial(block_kernel, lons, lats), out_shape=plt...  22.4 us
    unnamed x1, local copies, waits for them, and re-layouts  0.69 us

profile of v5, /device:TPU:8, one launch (start us, length us, event | category | flops | bytes accessed | tf_op | source)
XLA Modules:
  0.0 23.1 jit_solution(2942235802162946300)
XLA Ops:
  0.0 22.4 %swin_block.1 = bf16[12,18,4,128]{3,2,1,0:T(4,128)(2,1)S(1)} custom-call(bf16[12,18,4,128]{3,2,1,0:T(4,128)(2,1)} %bitcast.13, f32[192]{0:T(256)} %g1_hbm.1, bf16[192,576]{1,0:T(8,128)(2,1)} %wqkv_hbm.1, bf16[192,192]{1,0:T(8,128)(2,1)} %wproj_hbm.1, f32[12,2,20736]{2,1,0:T(2,128)} %bitcast.11, f32[192]{0:T(256)} %g2_hbm.1, bf16[192,768]{1,0:T(8,128)(2,1)} %w1_hbm.1, ...), custom_call_target="tpu_custom_call" | custom-call | tf_op jit(solution)/shard_map/swin_block/pallas_call | solution.py:300
  22.4 0.7 %copy.10 = bf16[4,12,2304]{2,0,1:T(4,128)(2,1)} copy(bf16[4,12,2304]{2,0,1:T(4,128)(2,1)S(1)} %bitcast.10) | data formatting | bytes 442368

commit v6 on v5

--- a/solution.py
+++ b/solution.py
@@ -28,9 +28,14 @@
     return jnp.dot(a, b, preferred_element_type=F32)
 
 
+def row_mean(values):
+    mean = dot(values.astype(BF16), jnp.ones((CH, 128), BF16)) * (1.0 / CH)
+    return jnp.concatenate([mean, mean[:, : CH - 128]], axis=1)
+
+
 def layer_norm(values, gain):
-    center = values - jnp.mean(values, axis=-1, keepdims=True)
-    spread = jnp.mean(center * center, axis=-1, keepdims=True)
+    center = values - row_mean(values)
+    spread = row_mean(center * center)
     return center * lax.rsqrt(spread + 1e-05) * gain
 
 
@@ -234,33 +239,36 @@
                 norm = jnp.where(head_of == h, total[h * HALF : (h + 1) * HALF], norm)
             mixs[rwin, zwin * HALF : (zwin + 1) * HALF, :] = mixed / norm
 
-    def finish(rwin, ew):
-        attn = dot(mixs[rwin].astype(BF16), wproj[...]).astype(BF16).astype(F32)
-        resid = (tokens(qlo, qhi, rwin * TOK, TOK) + attn).astype(BF16).astype(F32)
+    def finish(rwins, ew):
+        first, size = rwins[0] * TOK, len(rwins) * TOK
+        mixed = jnp.concatenate([mixs[rwin] for rwin in rwins], axis=0)
+        attn = dot(mixed.astype(BF16), wproj[...]).astype(BF16).astype(F32)
+        resid = (tokens(qlo, qhi, first, size) + attn).astype(BF16).astype(F32)
         normed = layer_norm(resid, g2[...]).astype(BF16)
         hidden = jax.nn.gelu(dot(normed, w1[...])).astype(BF16)
         result = resid + dot_nt(hidden, w2t[...])
-        rlo[...] = result[:, :128]
-        rhi[:, : CH - 128] = result[:, 128:]
-        for zwin in range(2):
-            for lev in range(2):
-                base = zwin * HALF + 36 * lev
-                even_lo = rlo[pl.ds(base, 18, stride=2), :]
-                even_hi = rhi[pl.ds(base, 18, stride=2), :]
-                odd_lo = pltpu.roll(rlo[pl.ds(base + 1, 18, stride=2), :], 64, 1)
-                odd_hi = pltpu.roll(rhi[pl.ds(base + 1, 18, stride=2), :], 64, 1)
-                dest = LEVEL[zwin][lev]
-                orow[pl.ds(dest, 18, stride=12), :] = even_lo
-                orow[pl.ds(dest + 4, 18, stride=12), :] = jnp.where(lane18 < 64, even_hi, odd_lo)
-                orow[pl.ds(dest + 8, 18, stride=12), :] = jnp.where(lane18 < 64, odd_lo, odd_hi)
-        tile = orow[...].reshape(6, 9, 4, 128).astype(BF16)
+        rlo[first : first + size, :] = result[:, :128]
+        rhi[first : first + size, : CH - 128] = result[:, 128:]
         columns = pl.ds(9 * ew, 9)
-        if rwin == 0:
-            out[3:9, columns] = tile
-        else:
-            out[9:12, columns] = tile[:3]
-            back[:, columns] = tile[3:]
-            give_back(ew).start()
+        for rwin in rwins:
+            for zwin in range(2):
+                for lev in range(2):
+                    base = rwin * TOK + zwin * HALF + 36 * lev
+                    even_lo = rlo[pl.ds(base, 18, stride=2), :]
+                    even_hi = rhi[pl.ds(base, 18, stride=2), :]
+                    odd_lo = pltpu.roll(rlo[pl.ds(base + 1, 18, stride=2), :], 64, 1)
+                    odd_hi = pltpu.roll(rhi[pl.ds(base + 1, 18, stride=2), :], 64, 1)
+                    dest = rwin * 216 + LEVEL[zwin][lev]
+                    orow[pl.ds(dest, 18, stride=12), :] = even_lo
+                    orow[pl.ds(dest + 4, 18, stride=12), :] = jnp.where(lane18 < 64, even_hi, odd_lo)
+                    orow[pl.ds(dest + 8, 18, stride=12), :] = jnp.where(lane18 < 64, odd_lo, odd_hi)
+            tile = orow[rwin * 216 : rwin * 216 + 216, :].reshape(6, 9, 4, 128).astype(BF16)
+            if rwin == 0:
+                out[3:9, columns] = tile
+            else:
+                out[9:12, columns] = tile[:3]
+                back[:, columns] = tile[3:]
+                give_back(ew).start()
 
     def arrive(which, rwin, ew):
         for side in range(2):
@@ -277,7 +285,7 @@
         queries(rwin, early)
         arrive(key_needs, rwin, early)
         attend(rwin, early)
-        finish(rwin, early)
+    finish((0, 1), early)
     for rwin in (1, 0):
         arrive(query_needs, rwin, late)
         queries(rwin, late)
@@ -285,7 +293,7 @@
     for rwin in (1, 0):
         arrive(key_needs, rwin, late)
         attend(rwin, late)
-        finish(rwin, late)
+        finish((rwin,), late)
     for copy in halo:
         copy.wait_send()
     for ew in range(2):
@@ -317,9 +325,9 @@
             pltpu.VMEM((576, 128), F32),
             pltpu.VMEM((576, 128), F32),
             pltpu.VMEM((2, TOK, CH), F32),
-            pltpu.VMEM((TOK, 128), F32),
-            pltpu.VMEM((TOK, 128), F32),
-            pltpu.VMEM((216, 128), F32),
+            pltpu.VMEM((2 * TOK, 128), F32),
+            pltpu.VMEM((2 * TOK, 128), F32),
+            pltpu.VMEM((432, 128), F32),
             pltpu.VMEM((3, 18, 4, 128), BF16),
             pltpu.VMEM((CH,), F32),
             pltpu.VMEM((CH,), F32),

time: 23.2 us -> 23 us (level)
  the two profiles are of different devices: /device:TPU:8 before, /device:TPU:1 now
where the time goes in v6:
time: 23 us; the launch traced here: 22.9 us
  Pallas kernels  22.2 us (97%)
  local copies, waits for them, and re-layouts  0.69 us (3%)
    pallas_call x1, Pallas kernels, shards(): pl.pallas_call(functools.partial(block_kernel, lons, lats), out_shape=plt...  22.2 us
    unnamed x1, local copies, waits for them, and re-layouts  0.69 us

profile of v6, /device:TPU:1, one launch (start us, length us, event | category | flops | bytes accessed | tf_op | source)
XLA Modules:
  0.0 22.9 jit_solution(2724068911448768364)
XLA Ops:
  0.0 22.2 %swin_block.1 = bf16[12,18,4,128]{3,2,1,0:T(4,128)(2,1)S(1)} custom-call(bf16[12,18,4,128]{3,2,1,0:T(4,128)(2,1)} %bitcast.13, f32[192]{0:T(256)} %g1_hbm.1, bf16[192,576]{1,0:T(8,128)(2,1)} %wqkv_hbm.1, bf16[192,192]{1,0:T(8,128)(2,1)} %wproj_hbm.1, f32[12,2,20736]{2,1,0:T(2,128)} %bitcast.11, f32[192]{0:T(256)} %g2_hbm.1, bf16[192,768]{1,0:T(8,128)(2,1)} %w1_hbm.1, ...), custom_call_target="tpu_custom_call" | custom-call | tf_op jit(solution)/shard_map/swin_block/pallas_call | solution.py:308
  22.2 0.7 %copy.10 = bf16[4,12,2304]{2,0,1:T(4,128)(2,1)} copy(bf16[4,12,2304]{2,0,1:T(4,128)(2,1)S(1)} %bitcast.10) | data formatting | bytes 442368

commit v7 on v6

--- a/solution.py
+++ b/solution.py
@@ -157,7 +157,7 @@
                 low = jnp.where(lanes < 128 - turn, this, following)
                 dest = (zwin * 2 + wc // 6) * 864 + 6 * odd + wc % 6
                 blo[pl.ds(dest, 72, stride=12), :] = low * LOG2E + pen_lo
-                bhi[pl.ds(dest, 72, stride=12), :] = following * LOG2E + pen_hi
+                bhi[pl.ds(dest, 72, stride=12), :] = jnp.where(lanes < TOK - 128, following * LOG2E + pen_hi, NEG)
 
     pl.semaphore_wait(ready.at[2], 1)
     for i in (6, 7):
@@ -224,11 +224,12 @@
                 xhi[pl.ds(dest + 1, 36, stride=2), :] = r2
         normed = layer_norm(tokens(xlo, xhi, rwin * 2 * TOK, 2 * TOK), g1[...]).astype(BF16)
         kv = dot(normed, wqkv[:, CH:]).astype(BF16)
+        blank = jnp.zeros((256 - TOK, 2 * CH), BF16)
         for zwin in range(2):
-            mine = kv[zwin * TOK : (zwin + 1) * TOK]
+            mine = jnp.concatenate([kv[zwin * TOK : (zwin + 1) * TOK], blank], axis=0)
             scores = dot_nt(qst[rwin, zwin], mine[:, :CH])
             brow = pl.ds(pl.multiple_of(((zwin * 2 + 1 - ew) * 2 + rwin) * 432, 8), 432)
-            scores = scores + jnp.concatenate([blo[brow, :], bhi[brow, :][:, :16]], axis=1)
+            scores = scores + jnp.concatenate([blo[brow, :], bhi[brow, :]], axis=1)
             top = jnp.max(scores, axis=-1, keepdims=True)
             probs = jnp.exp2(scores - top)
             total = jnp.sum(probs, axis=-1, keepdims=True)

time: 23 us -> 22.9 us (level)
  no operation moved by 1% of the time
where the time goes in v7:
time: 22.9 us; the launch traced here: 22.8 us
  Pallas kernels  22.1 us (97%)
  local copies, waits for them, and re-layouts  0.69 us (3%)
    pallas_call x1, Pallas kernels, shards(): pl.pallas_call(functools.partial(block_kernel, lons, lats), out_shape=plt...  22.1 us
    unnamed x1, local copies, waits for them, and re-layouts  0.69 us

profile of v7, /device:TPU:1, one launch (start us, length us, event | category | flops | bytes accessed | tf_op | source)
XLA Modules:
  0.0 22.8 jit_solution(1607725279405709370)
XLA Ops:
  0.0 22.1 %swin_block.1 = bf16[12,18,4,128]{3,2,1,0:T(4,128)(2,1)S(1)} custom-call(bf16[12,18,4,128]{3,2,1,0:T(4,128)(2,1)} %bitcast.13, f32[192]{0:T(256)} %g1_hbm.1, bf16[192,576]{1,0:T(8,128)(2,1)} %wqkv_hbm.1, bf16[192,192]{1,0:T(8,128)(2,1)} %wproj_hbm.1, f32[12,2,20736]{2,1,0:T(2,128)} %bitcast.11, f32[192]{0:T(256)} %g2_hbm.1, bf16[192,768]{1,0:T(8,128)(2,1)} %w1_hbm.1, ...), custom_call_target="tpu_custom_call" | custom-call | tf_op jit(solution)/shard_map/swin_block/pallas_call | solution.py:309
  22.1 0.7 %copy.10 = bf16[4,12,2304]{2,0,1:T(4,128)(2,1)} copy(bf16[4,12,2304]{2,0,1:T(4,128)(2,1)S(1)} %bitcast.10) | data formatting | bytes 442368

commit v8 on v7

--- a/solution.py
+++ b/solution.py
@@ -106,9 +106,10 @@
 
     def westward():
         pl.semaphore_wait(ready.at[0], 1)
+        for i in (4, 3):
+            halo[i].start()
         pl.semaphore_wait(ready.at[1], 1)
-        for i in (3, 4, 5):
-            halo[i].start()
+        halo[5].start()
 
     loads[0].wait()
 

time: 22.9 us -> 22.9 us (level)
  the two profiles are of different devices: /device:TPU:1 before, /device:TPU:8 now
where the time goes in v8:
time: 22.9 us; the launch traced here: 22.8 us
  Pallas kernels  22.1 us (97%)
  local copies, waits for them, and re-layouts  0.69 us (3%)
    pallas_call x1, Pallas kernels, shards(): pl.pallas_call(functools.partial(block_kernel, lons, lats), out_shape=plt...  22.1 us
    unnamed x1, local copies, waits for them, and re-layouts  0.69 us

profile of v8, /device:TPU:8, one launch (start us, length us, event | category | flops | bytes accessed | tf_op | source)
XLA Modules:
  0.0 22.8 jit_solution(2520095412873630400)
XLA Ops:
  0.0 22.1 %swin_block.1 = bf16[12,18,4,128]{3,2,1,0:T(4,128)(2,1)S(1)} custom-call(bf16[12,18,4,128]{3,2,1,0:T(4,128)(2,1)} %bitcast.13, f32[192]{0:T(256)} %g1_hbm.1, bf16[192,576]{1,0:T(8,128)(2,1)} %wqkv_hbm.1, bf16[192,192]{1,0:T(8,128)(2,1)} %wproj_hbm.1, f32[12,2,20736]{2,1,0:T(2,128)} %bitcast.11, f32[192]{0:T(256)} %g2_hbm.1, bf16[192,768]{1,0:T(8,128)(2,1)} %w1_hbm.1, ...), custom_call_target="tpu_custom_call" | custom-call | tf_op jit(solution)/shard_map/swin_block/pallas_call | solution.py:310
  22.1 0.7 %copy.10 = bf16[4,12,2304]{2,0,1:T(4,128)(2,1)} copy(bf16[4,12,2304]{2,0,1:T(4,128)(2,1)S(1)} %bitcast.10) | data formatting | bytes 442368

commit v9 on v8

--- a/solution.py
+++ b/solution.py
@@ -164,10 +164,6 @@
     for i in (6, 7):
         halo[i].start()
     across = lax.rem(lon, 16) == 0
-
-    @pl.when(jnp.logical_not(across))
-    def _():
-        westward()
 
     for copy in loads[1:]:
         copy.wait()
@@ -282,9 +278,16 @@
 
     early = jnp.where(across, 1, 0)
     late = 1 - early
+    queries(0, early)
+
+    @pl.when(jnp.logical_not(across))
+    def _():
+        westward()
+
     for rwin in range(2):
-        arrive(query_needs, rwin, early)
-        queries(rwin, early)
+        if rwin:
+            arrive(query_needs, rwin, early)
+            queries(rwin, early)
         arrive(key_needs, rwin, early)
         attend(rwin, early)
     finish((0, 1), early)

time: 22.9 us -> 22.9 us (level)
  the two profiles are of different devices: /device:TPU:8 before, /device:TPU:1 now
where the time goes in v9:
time: 22.9 us; the launch traced here: 22.8 us
  Pallas kernels  22.1 us (97%)
  local copies, waits for them, and re-layouts  0.69 us (3%)
    pallas_call x1, Pallas kernels, shards(): pl.pallas_call(functools.partial(block_kernel, lons, lats), out_shape=plt...  22.1 us
    unnamed x1, local copies, waits for them, and re-layouts  0.69 us

profile of v9, /device:TPU:1, one launch (start us, length us, event | category | flops | bytes accessed | tf_op | source)
XLA Modules:
  0.0 22.8 jit_solution(12738565830425929954)
XLA Ops:
  0.0 22.1 %swin_block.1 = bf16[12,18,4,128]{3,2,1,0:T(4,128)(2,1)S(1)} custom-call(bf16[12,18,4,128]{3,2,1,0:T(4,128)(2,1)} %bitcast.13, f32[192]{0:T(256)} %g1_hbm.1, bf16[192,576]{1,0:T(8,128)(2,1)} %wqkv_hbm.1, bf16[192,192]{1,0:T(8,128)(2,1)} %wproj_hbm.1, f32[12,2,20736]{2,1,0:T(2,128)} %bitcast.11, f32[192]{0:T(256)} %g2_hbm.1, bf16[192,768]{1,0:T(8,128)(2,1)} %w1_hbm.1, ...), custom_call_target="tpu_custom_call" | custom-call | tf_op jit(solution)/shard_map/swin_block/pallas_call | solution.py:313
  22.1 0.7 %copy.10 = bf16[4,12,2304]{2,0,1:T(4,128)(2,1)} copy(bf16[4,12,2304]{2,0,1:T(4,128)(2,1)S(1)} %bitcast.10) | data formatting | bytes 442368

commit v10 on v8

--- a/solution.py
+++ b/solution.py
@@ -268,9 +268,9 @@
             if rwin == 0:
                 out[3:9, columns] = tile
             else:
-                out[9:12, columns] = tile[:3]
                 back[:, columns] = tile[3:]
                 give_back(ew).start()
+                out[9:12, columns] = tile[:3]
 
     def arrive(which, rwin, ew):
         for side in range(2):

time: 22.9 us -> 22.9 us (level)
  the two profiles are of different devices: /device:TPU:8 before, /device:TPU:1 now
where the time goes in v10:
time: 22.9 us; the launch traced here: 22.8 us
  Pallas kernels  22.1 us (97%)
  local copies, waits for them, and re-layouts  0.69 us (3%)
    pallas_call x1, Pallas kernels, shards(): pl.pallas_call(functools.partial(block_kernel, lons, lats), out_shape=plt...  22.1 us
    unnamed x1, local copies, waits for them, and re-layouts  0.69 us

profile of v10, /device:TPU:1, one launch (start us, length us, event | category | flops | bytes accessed | tf_op | source)
XLA Modules:
  0.0 22.8 jit_solution(9183459174463405480)
XLA Ops:
  0.0 22.1 %swin_block.1 = bf16[12,18,4,128]{3,2,1,0:T(4,128)(2,1)S(1)} custom-call(bf16[12,18,4,128]{3,2,1,0:T(4,128)(2,1)} %bitcast.13, f32[192]{0:T(256)} %g1_hbm.1, bf16[192,576]{1,0:T(8,128)(2,1)} %wqkv_hbm.1, bf16[192,192]{1,0:T(8,128)(2,1)} %wproj_hbm.1, f32[12,2,20736]{2,1,0:T(2,128)} %bitcast.11, f32[192]{0:T(256)} %g2_hbm.1, bf16[192,768]{1,0:T(8,128)(2,1)} %w1_hbm.1, ...), custom_call_target="tpu_custom_call" | custom-call | tf_op jit(solution)/shard_map/swin_block/pallas_call | solution.py:310
  22.1 0.7 %copy.10 = bf16[4,12,2304]{2,0,1:T(4,128)(2,1)} copy(bf16[4,12,2304]{2,0,1:T(4,128)(2,1)S(1)} %bitcast.10) | data formatting | bytes 442368
